TPU v7x, 32 devices: a whole 2x2x4 slice. The times are simulated.
32 devices in a mesh: dp: 16 (over z, y, core), seq: 2 (over x).
Axes of the slice: x: 2, y: 2, z: 4, core: 2. Of those that a mesh axis runs over, the one named last changes fastest.
Arguments:
- inputs: float32 [16, 256, 640], P('dp', 'seq'), may hold values from -6 to 6
- positions: int32 [16, 256], P('dp'), may hold values from 0 to 1277, as said below
- cotangent: float32 [16, 256, 640], P('dp', 'seq'), may hold values from -16 to 16
- q_weight: bfloat16 [1024, 640], P(('dp', 'seq')), may hold values from -0.5 to 0.5
- k_weight: bfloat16 [256, 640], P(('dp', 'seq')), may hold values from -0.5 to 0.5
- v_weight: bfloat16 [256, 640], P(('dp', 'seq')), may hold values from -0.25 to 0.25
- o_weight: bfloat16 [1024, 640], P(('dp', 'seq')), may hold values from -0.1875 to 0.1875
- gate_weight: bfloat16 [2048, 640], P(('dp', 'seq')), may hold values from -0.25 to 0.25
- up_weight: bfloat16 [2048, 640], P(('dp', 'seq')), may hold values from -0.25 to 0.25
- down_weight: bfloat16 [2048, 640], P(('dp', 'seq')), may hold values from -0.125 to 0.125
- norm_gains: bfloat16 [3072], P(('dp', 'seq')), may hold values from 0.5 to 1.5
Outputs:
- output: float32 [16, 256, 640], P('dp', 'seq')
- input_grad: float32 [16, 256, 640], P('dp', 'seq')
- q_grad: float32 [1024, 640], P(('dp', 'seq'))
- k_grad: float32 [256, 640], P(('dp', 'seq'))
- v_grad: float32 [256, 640], P(('dp', 'seq'))
- o_grad: float32 [1024, 640], P(('dp', 'seq'))
- gate_grad: float32 [2048, 640], P(('dp', 'seq'))
- up_grad: float32 [2048, 640], P(('dp', 'seq'))
- down_grad: float32 [2048, 640], P(('dp', 'seq'))
- gains_grad: float32 [3072], P(('dp', 'seq'))
Inputs may be any that keep to these rules, and one draw needn't show every extreme that they name: Along a row, positions rise by one from token to token, except where a new document begins and they restart at 0; every row has at least one such restart after its first token.
All inputs are finite; a program needn't handle non-finite values.
Results may differ from a plain program's by a relative error of at most 0.014.
Values may be sent and summed in bfloat16 or wider, within the bound.
A program may use at most 128 MiB of HBM per device.

v0:
```python
import jax
import jax.numpy as jnp
from jax import lax
from jax.sharding import PartitionSpec as P

D = 640
HQ = 4
HD = 256
WIN = 512


EPSILON = 1e-06


def shifted(block, axis, distance):
    devices = range(lax.axis_size(axis))
    route = [(i - distance, i) for i in devices if i - distance in devices]
    return lax.ppermute(block, axis, route)


def rms_scale(values, scales):
    inverse = lax.rsqrt(jnp.mean(values * values, axis=-1, keepdims=True) + EPSILON)
    return values * inverse * scales


def rotary_tables(positions):
    half_size = HD // 2
    frequency = 10000.0 ** (-2.0 * jnp.arange(half_size, dtype=jnp.float32) / HD)
    angles = positions.astype(jnp.float32)[:, None] * frequency[None, :]
    angles = jnp.concatenate([angles, angles], axis=-1)
    return (jnp.cos(angles), jnp.sin(angles))


def norm_rotate(raw_values, scales, cos_table, sin_table):
    normed = rms_scale(raw_values, scales)
    front_half = normed[..., : HD // 2]
    back_half = normed[..., HD // 2 :]
    turned = jnp.concatenate([-back_half, front_half], axis=-1)
    return normed * cos_table[:, None, :] + turned * sin_table[:, None, :]


def window_mask(query_pos, key_pos, query_idx, key_idx):
    spacing = query_pos[:, None] - key_pos[None, :]
    return (spacing == query_idx[:, None] - key_idx[None, :]) & (spacing >= 0) & (spacing < WIN)


def glu_product(gate_pre, up_pre):
    return jax.nn.gelu(gate_pre, approximate=True) * up_pre


def split_gains(gains_all):
    return (
        gains_all[0:D],
        gains_all[D : 2 * D],
        gains_all[2 * D : 3 * D],
        gains_all[3 * D : 4 * D],
        gains_all[4 * D : 4 * D + HD],
        gains_all[4 * D + HD : 4 * D + 2 * HD],
    )


def times_rows(left, weight):
    return lax.dot_general(
        left, weight, (((1,), (1,)), ((), ())), preferred_element_type=jnp.float32
    )


def times_plain(left, weight):
    return jnp.dot(left, weight, preferred_element_type=jnp.float32)


def outer_sum(left, right):
    return lax.dot_general(
        left, right, (((0,), (0,)), ((), ())), preferred_element_type=jnp.float32
    )


def score_rows(query_rows, key_rows, allowed, factor):
    raw_scores = factor * times_rows(query_rows, key_rows)
    by_head = raw_scores.reshape(-1, allowed.shape[0], allowed.shape[1])
    return jnp.where(allowed[None], by_head, -1e30).reshape(raw_scores.shape)


def packed_term(entries, gain_terms, gain_share, per_device, count):
    groups = count // per_device
    blocks = []
    for left, right, width in entries:
        blocks.append(outer_sum(left, right).reshape(groups, width, D))
    portion = gain_terms
    portion = jnp.pad(portion.reshape(groups, 1, gain_share), ((0, 0), (0, 0), (0, D - gain_share)))
    blocks.append(portion)
    return jnp.concatenate(blocks, axis=1).reshape(groups * per_device, D)


def unpack_rows(summed, widths):
    pieces = []
    offset = 0
    for width in widths:
        pieces.append(summed[offset : offset + width])
        offset = offset + width
    return pieces


def on_device(
    inputs,
    positions,
    cotangent,
    q_weight,
    k_weight,
    v_weight,
    o_weight,
    gate_weight,
    up_weight,
    down_weight,
    norm_gains,
):
    tokens_here = inputs.shape[1]
    scale = HD ** (-0.5)
    block_index = lax.axis_index("seq")
    shards = (
        q_weight,
        k_weight,
        v_weight,
        o_weight,
        gate_weight,
        up_weight,
        down_weight,
        norm_gains,
    )
    width_query = q_weight.shape[0]
    width_key = k_weight.shape[0]
    width_ffn = gate_weight.shape[0]
    gain_share = norm_gains.shape[0]
    gathered = (
        lax.all_gather(shards[0], ("dp", "seq"), axis=0, tiled=True),
        lax.all_gather(shards[1], ("dp", "seq"), axis=0, tiled=True),
        lax.all_gather(shards[2], ("dp", "seq"), axis=0, tiled=True),
        lax.all_gather(shards[3], ("dp", "seq"), axis=0, tiled=True),
        lax.all_gather(shards[4], ("dp", "seq"), axis=0, tiled=True),
        lax.all_gather(shards[5], ("dp", "seq"), axis=0, tiled=True),
        lax.all_gather(shards[6], ("dp", "seq"), axis=0, tiled=True),
        lax.all_gather(shards[7], ("dp", "seq"), axis=0, tiled=True),
    )
    w_query, w_key, w_value, w_out, w_gate, w_upper, w_down = gathered[:7]
    gain_in, gain_attn, gain_pre, gain_post, gain_query, gain_key = split_gains(
        gathered[7].astype(jnp.float32)
    )
    seq_inputs = inputs[0]
    seq_cotangent = cotangent[0]
    every_pos = positions[0]
    own_pos = lax.dynamic_slice_in_dim(every_pos, block_index * tokens_here, tokens_here)
    prior_pos = lax.dynamic_slice_in_dim(
        every_pos, jnp.maximum(block_index - 1, 0) * tokens_here, tokens_here
    )
    query_idx = block_index * tokens_here + jnp.arange(tokens_here, dtype=jnp.int32)
    key_idx = (block_index - 1) * tokens_here + jnp.arange(2 * tokens_here, dtype=jnp.int32)
    allowed = window_mask(own_pos, jnp.concatenate([prior_pos, own_pos]), query_idx, key_idx)
    allowed = allowed & (key_idx >= 0)[None, :]
    cos_table, sin_table = rotary_tables(own_pos)
    normed_in = rms_scale(seq_inputs, gain_in).astype(jnp.bfloat16)
    queries_raw = times_rows(normed_in, w_query).reshape(tokens_here, HQ, HD)
    keys_raw = times_rows(normed_in, w_key).reshape(tokens_here, 1, HD)
    values_raw = times_rows(normed_in, w_value)
    queries_rot = norm_rotate(queries_raw, gain_query, cos_table, sin_table).astype(jnp.bfloat16)
    keys_rot = norm_rotate(keys_raw, gain_key, cos_table, sin_table)[:, 0].astype(jnp.bfloat16)
    values_b = values_raw.astype(jnp.bfloat16)
    prior_keys, prior_values = shifted((keys_rot, values_b), "seq", 1)
    key_rows = jnp.concatenate([prior_keys, keys_rot], axis=0)
    value_rows = jnp.concatenate([prior_values, values_b], axis=0)
    query_rows = jnp.transpose(queries_rot, (1, 0, 2)).reshape(HQ * tokens_here, HD)
    scores = score_rows(query_rows, key_rows, allowed, scale)
    highest = jnp.max(scores, axis=-1, keepdims=True)
    log_total = highest + jnp.log(jnp.sum(jnp.exp(scores - highest), axis=-1, keepdims=True))
    probs_b = jnp.exp(scores - log_total).astype(jnp.bfloat16)
    attended = times_plain(probs_b, value_rows).astype(jnp.bfloat16)
    merged = jnp.transpose(attended.reshape(HQ, tokens_here, HD), (1, 0, 2)).reshape(
        tokens_here, HQ * HD
    )
    branch = times_plain(merged, w_out)
    middle = seq_inputs + rms_scale(branch, gain_attn)
    normed_ff = rms_scale(middle, gain_pre).astype(jnp.bfloat16)
    gate_pre = times_rows(normed_ff, w_gate)
    up_pre = times_rows(normed_ff, w_upper)
    hidden = glu_product(gate_pre, up_pre).astype(jnp.bfloat16)
    ffn_out = times_plain(hidden, w_down)
    output = middle + rms_scale(ffn_out, gain_post)
    regathered = (
        lax.all_gather(shards[0], ("dp", "seq"), axis=0, tiled=True),
        lax.all_gather(shards[1], ("dp", "seq"), axis=0, tiled=True),
        lax.all_gather(shards[2], ("dp", "seq"), axis=0, tiled=True),
        lax.all_gather(shards[3], ("dp", "seq"), axis=0, tiled=True),
        lax.all_gather(shards[4], ("dp", "seq"), axis=0, tiled=True),
        lax.all_gather(shards[5], ("dp", "seq"), axis=0, tiled=True),
        lax.all_gather(shards[6], ("dp", "seq"), axis=0, tiled=True),
        lax.all_gather(shards[7], ("dp", "seq"), axis=0, tiled=True),
    )
    w_query, w_key, w_value, w_out, w_gate, w_upper, w_down = regathered[:7]
    gain_in, gain_attn, gain_pre, gain_post, gain_query, gain_key = split_gains(
        regathered[7].astype(jnp.float32)
    )
    unused, pull = jax.vjp(rms_scale, ffn_out, gain_post)
    d_ffn, grad_post = pull(seq_cotangent)
    d_ffn = d_ffn.astype(jnp.bfloat16)
    d_hidden = times_rows(d_ffn, w_down)
    unused, pull = jax.vjp(glu_product, gate_pre, up_pre)
    d_gate, d_up = pull(d_hidden)
    d_gate = d_gate.astype(jnp.bfloat16)
    d_up = d_up.astype(jnp.bfloat16)
    d_normed_ff = times_plain(d_gate, w_gate) + times_plain(d_up, w_upper)
    ffn_entries = [
        (d_gate, normed_ff, width_ffn),
        (d_up, normed_ff, width_ffn),
        (hidden, d_ffn, width_ffn),
    ]
    unused, pull = jax.vjp(rms_scale, middle, gain_pre)
    d_mid_norm, grad_pre = pull(d_normed_ff)
    d_middle = seq_cotangent + d_mid_norm
    unused, pull = jax.vjp(rms_scale, branch, gain_attn)
    d_branch, grad_attn = pull(d_middle)
    d_branch = d_branch.astype(jnp.bfloat16)
    d_merged = times_rows(d_branch, w_out).astype(jnp.bfloat16)
    d_rows = jnp.transpose(d_merged.reshape(tokens_here, HQ, HD), (1, 0, 2)).reshape(
        HQ * tokens_here, HD
    )
    probs = jnp.exp(score_rows(query_rows, key_rows, allowed, scale) - log_total)
    probs_again = probs.astype(jnp.bfloat16)
    delta = jnp.sum(
        d_rows.astype(jnp.float32) * attended.astype(jnp.float32), axis=-1, keepdims=True
    )
    d_probs = times_rows(d_rows, value_rows)
    d_scores = (probs * (d_probs - delta)).astype(jnp.bfloat16)
    d_query_rows = scale * times_plain(d_scores, key_rows)
    d_key_rows = scale * outer_sum(d_scores, query_rows)
    d_value_rows = outer_sum(probs_again, d_rows)
    sent_keys, sent_values = (
        shifted(d_key_rows[:tokens_here].astype(jnp.bfloat16), "seq", -1).astype(jnp.float32),
        shifted(d_value_rows[:tokens_here].astype(jnp.bfloat16), "seq", -1).astype(jnp.float32),
    )
    d_keys_rot = d_key_rows[tokens_here:] + sent_keys
    d_values = (d_value_rows[tokens_here:] + sent_values).astype(jnp.bfloat16)
    d_queries_rot = jnp.transpose(d_query_rows.reshape(HQ, tokens_here, HD), (1, 0, 2))

    def rotate_all(raw_values, scales):
        return norm_rotate(raw_values, scales, cos_table, sin_table)

    unused, pull = jax.vjp(rotate_all, queries_raw, gain_query)
    d_queries, grad_query = pull(d_queries_rot)
    unused, pull = jax.vjp(rotate_all, keys_raw, gain_key)
    d_keys, grad_key = pull(d_keys_rot[:, None, :])
    d_queries = d_queries.reshape(tokens_here, HQ * HD).astype(jnp.bfloat16)
    d_keys = d_keys.reshape(tokens_here, HD).astype(jnp.bfloat16)
    d_normed_in = (
        times_plain(d_queries, w_query)
        + times_plain(d_keys, w_key)
        + times_plain(d_values, w_value)
    )
    unused, pull = jax.vjp(rms_scale, seq_inputs, gain_in)
    d_in_norm, grad_in = pull(d_normed_in)
    input_grad = d_middle + d_in_norm
    gains_grad = jnp.concatenate([grad_in, grad_attn, grad_pre, grad_post, grad_query, grad_key])
    attn_entries = [
        (d_queries, normed_in, width_query),
        (d_keys, normed_in, width_key),
        (d_values, normed_in, width_key),
        (merged, d_branch, width_query),
    ]
    attn_widths = [width_query, width_key, width_key, width_query]
    all_rows = 2 * width_query + 2 * width_key + 3 * width_ffn + 1
    summed = lax.psum_scatter(
        packed_term(
            attn_entries + ffn_entries,
            gains_grad,
            gain_share,
            all_rows,
            lax.axis_size(("dp", "seq")) * all_rows,
        ),
        ("dp", "seq"),
        scatter_dimension=0,
        tiled=True,
    )
    parts = unpack_rows(summed, attn_widths + [width_ffn, width_ffn, width_ffn, 1])
    results = tuple(parts[:7]) + (parts[7][0, :gain_share],)
    return (output[None], input_grad[None]) + results


def solution(mesh):
    return jax.shard_map(
        on_device,
        mesh=mesh,
        in_specs=(
            P("dp", "seq", None),
            P("dp", None),
            P("dp", "seq", None),
            P(("dp", "seq"), None),
            P(("dp", "seq"), None),
            P(("dp", "seq"), None),
            P(("dp", "seq"), None),
            P(("dp", "seq"), None),
            P(("dp", "seq"), None),
            P(("dp", "seq"), None),
            P(("dp", "seq")),
        ),
        out_specs=(
            P("dp", "seq", None),
            P("dp", "seq", None),
            P(("dp", "seq"), None),
            P(("dp", "seq"), None),
            P(("dp", "seq"), None),
            P(("dp", "seq"), None),
            P(("dp", "seq"), None),
            P(("dp", "seq"), None),
            P(("dp", "seq"), None),
            P(("dp", "seq")),
        ),
        check_vma=False,
    )
```

profile of v0, /device:TPU:0, one launch (start us, length us, event | category | flops | bytes accessed | tf_op | source)
XLA Modules:
  0.0 770.8 jit_solution(11348658370322643858)
XLA Ops:
  8.0 0.7 all-gather.8.cloned.1.call-update
  10.0 0.9 dynamic-update-slice
  10.9 42.1 %all-reduce.5 = bf16[3072]{0:T(1024)(128)(2,1)S(1)} all-reduce(bf16[3072]{0:T(1024)(128)(2,1)S(1)} %dynamic-update-slice), channel_id=1, replica_groups=mesh['dp'=16,'seq'=2] {'dp','seq'}, use_global_device_ids=true, to_apply=%add.5 | all-reduce | flops 3072 | bytes 12288
  53.0 1.1 fusion.21
  54.1 68.4 %all_gather.35 = bf16[256,640]{1,0:T(8,128)(2,1)S(1)} all-gather(bf16[8,640]{1,0:T(8,128)(2,1)} %param.16), channel_id=1, replica_groups=mesh['dp'=16,'seq'=2] {'dp','seq'}, dimensions={0}, use_global_device_ids=true | all-gather | bytes 337920 | tf_op jit(solution)/shard_map/all_gather | solution.py:137
  123.2 1.2 convolution_convert_fusion.2
  124.4 1.7 collective-permute-start.1
  126.2 66.4 %all_gather.34 = bf16[256,640]{1,0:T(8,128)(2,1)S(1)} all-gather(bf16[8,640]{1,0:T(8,128)(2,1)} %param.15), channel_id=1, replica_groups=mesh['dp'=16,'seq'=2] {'dp','seq'}, dimensions={0}, use_global_device_ids=true | all-gather | bytes 337920 | tf_op jit(solution)/shard_map/all_gather | solution.py:136
  192.6 1.4 multiply_reduce_fusion.13
  194.7 0.7 fusion.61
  196.1 3.8 collective-permute-start
  200.2 1.1 fusion.23
  201.3 2.0 multiply_reduce_fusion.3
  205.2 1.9 multiply_reduce_fusion.12
  208.1 3.7 fusion.65
  211.8 32.8 %all-gather.12.cloned.1.call-done = bf16[2048,640]{1,0:T(8,128)(2,1)} async-done(((bf16[64,640]{1,0:T(8,128)(2,1)}), bf16[2048,640]{1,0:T(8,128)(2,1)}) %all-gather.12.cloned.1.call-update) | async-done | bytes 2621456 | tf_op jit(solution)/shard_map/all_gather | solution.py:140
  244.6 4.0 multiply_convert_fusion.1
  248.6 55.4 %all-gather.14.cloned.1.call-done = bf16[2048,640]{1,0:T(8,128)(2,1)} async-done(((bf16[64,640]{1,0:T(8,128)(2,1)}), bf16[2048,640]{1,0:T(8,128)(2,1)}) %all-gather.14.cloned.1.call-update) | async-done | bytes 2621456 | tf_op jit(solution)/shard_map/all_gather | solution.py:141
  303.9 2.4 multiply_reduce_fusion.10
  306.4 0.7 fusion.20
  307.1 0.9 fusion.15
  308.0 3.3 fusion.70
  311.6 1.4 multiply_convert_fusion
  313.0 3.2 fusion.68
  316.2 3.5 fusion.69
  320.4 1.2 multiply_reduce_fusion.4
  321.7 0.8 multiply_reduce_fusion.5
  323.4 1.0 fusion.37
  324.7 0.9 convolution_multiply_fusion.2
  325.6 1.1 convolution_multiply_fusion
  326.7 1.3 copy.39
  328.1 1.0 multiply_bitcast_fusion
  329.1 1.8 multiply_reduce_fusion
  332.0 1.0 slice.132
  333.0 1.3 collective-permute-start.2
  334.3 1.5 slice.131
  335.8 1.5 collective-permute-start.3
  337.3 2.0 convolution_dynamic-update-slice_fusion.1
  339.3 1.4 fusion.67
  340.8 1.4 multiply_bitcast_fusion.1
  342.2 1.2 fusion.31
  344.1 0.7 fusion.25
  345.2 1.4 multiply_reduce_fusion.6
  346.6 1.3 constant_dynamic-update-slice_fusion
  347.9 1.3 constant_dynamic-update-slice_fusion.8
  349.2 1.3 constant_dynamic-update-slice_fusion.7
  350.5 1.3 constant_dynamic-update-slice_fusion.6
  351.8 1.3 constant_dynamic-update-slice_fusion.5
  353.1 1.3 constant_dynamic-update-slice_fusion.4
  354.4 0.8 reshape.447
  355.2 1.1 convolution_dynamic-update-slice_fusion.3
  356.4 2.1 convolution_dynamic-update-slice_fusion.2
  358.5 3.2 convolution_dynamic-update-slice_fusion
  361.6 5.6 constant_dynamic-update-slice_fusion.3
  367.3 2.7 constant_dynamic-update-slice_fusion.2
  370.0 2.7 constant_dynamic-update-slice_fusion.1
  372.7 3.0 dynamic-update-slice.8
  375.7 23.7 %reshape.448 = f32[8736,640]{1,0:T(8,128)} reshape(f32[32,273,640]{2,1,0:T(8,128)} %dynamic-update-slice.8) | data formatting | bytes 44728320 | tf_op jit(solution)/shard_map/reshape | solution.py:92
  400.4 0.8 fusion.19
  401.2 356.6 %all-reduce.9.cloned.1.call-done = f32[8736,640]{1,0:T(8,128)} async-done(((f32[8736,640]{1,0:T(8,128)}), f32[8736,640]{1,0:T(8,128)}) %all-reduce.9.cloned.1.call-update) | async-done | bytes 22364176
  757.8 1.6 constant_dynamic-slice_fusion.3
  759.4 1.2 fusion.45
  760.6 1.5 constant_dynamic-slice_fusion.4
  762.1 1.9 constant_dynamic-slice_fusion
  (181 shorter events, 12.4 us)
Async XLA Ops:
  7.2 194.1 %all-gather.6.cloned.1.call-start = ((), (), s32[]{:S(2)}) async-start(), calls=%async_computation | async-start | bytes 1351680 | tf_op jit(solution)/shard_map/all_gather | solution.py:135
  7.9 197.2 %all-gather.8.cloned.1.call-start = ((), (), s32[]{:S(2)}) async-start(), calls=%async_computation.1 | async-start | bytes 1351680 | tf_op jit(solution)/shard_map/all_gather | solution.py:138
  8.7 199.4 %all-gather.10.cloned.1.call-start = ((), (), s32[]{:S(2)}) async-start(), calls=%async_computation.2 | async-start | bytes 2703360 | tf_op jit(solution)/shard_map/all_gather | solution.py:139
  9.4 235.2 %all-gather.12.cloned.1.call-start = ((), (), s32[]{:S(2)}) async-start(), calls=%async_computation.3 | async-start | bytes 2703360 | tf_op jit(solution)/shard_map/all_gather | solution.py:140
  10.0 293.9 %all-gather.14.cloned.1.call-start = ((), (), s32[]{:S(2)}) async-start(), calls=%async_computation.4 | async-start | bytes 2703360 | tf_op jit(solution)/shard_map/all_gather | solution.py:141
  54.1 149.4 %copy-start.45 = (f32[128]{0:T(128)}, f32[128]{0:T(128)S(1)}, u32[]{:S(2)}) copy-start(f32[128]{0:T(128)S(1)} %fusion.21) | copy-start | bytes 1540
  122.5 3.7 copy-start.11
  122.5 81.0 %copy-start.38 = (f32[128]{0:T(128)}, f32[128]{0:T(128)S(1)}, u32[]{:S(2)}) copy-start(f32[128]{0:T(128)S(1)} %fusion.46) | copy-start | bytes 1540
  124.4 80.2 %collective-permute-start.1 = (bf16[128,256]{1,0:T(8,128)(2,1)S(1)}, bf16[128,256]{1,0:T(8,128)(2,1)S(1)}, u32[]{:S(2)}, u32[]{:S(2)}) collective-permute-start(bf16[128,256]{1,0:T(8,128)(2,1)S(1)} %convolution_convert_fusion.2), channel_id=1, source_target_pairs={{0,1},{2,3},{4,5},{6,7},{8,9},{10,11},{12,13},{14,15},{16,17},{18,... | collective-permute-start | bytes 196616 | tf_op jit(solution)/shard_map/ppermute | solution.py:18
  126.1 631.7 %all-reduce.9.cloned.1.call-start = ((), (), s32[]{:S(2)}) async-start(), calls=%async_computation.5 | async-start | bytes 44728320
  126.1 73.8 %copy-start.31 = (f32[256]{0:T(256)}, f32[256]{0:T(256)S(1)}, u32[]{:S(2)}) copy-start(f32[256]{0:T(256)S(1)} %get-tuple-element.55) | copy-start | bytes 3076
  126.2 78.4 %copy-start.33 = (f32[256]{0:T(256)}, f32[256]{0:T(256)S(1)}, u32[]{:S(2)}) copy-start(f32[256]{0:T(256)S(1)} %get-tuple-element.56) | copy-start | bytes 3076
  192.6 8.7 %copy-start.9 = (bf16[256,640]{1,0:T(8,128)(2,1)}, bf16[256,640]{1,0:T(8,128)(2,1)S(1)}, u32[]{:S(2)}) copy-start(bf16[256,640]{1,0:T(8,128)(2,1)S(1)} %all_gather.34) | copy-start | bytes 983044
  194.0 0.6 copy-start.47
  194.0 5.9 copy-start.40
  196.0 8.6 %copy-start.18 = (f32[128,256]{1,0:T(8,128)}, f32[128,256]{1,0:T(8,128)S(1)}, u32[]{:S(2)}) copy-start(f32[128,256]{1,0:T(8,128)S(1)} %get-tuple-element.49) | copy-start | bytes 393220
  196.0 11.0 %copy-start.17 = (f32[128,256]{1,0:T(8,128)}, f32[128,256]{1,0:T(8,128)S(1)}, u32[]{:S(2)}) copy-start(f32[128,256]{1,0:T(8,128)S(1)} %get-tuple-element.50) | copy-start | bytes 393220
  196.1 11.0 %copy-start.24 = (bf16[128,256]{1,0:T(8,128)(2,1)}, bf16[128,256]{1,0:T(8,128)(2,1)S(1)}, u32[]{:S(2)}) copy-start(bf16[128,256]{1,0:T(8,128)(2,1)S(1)} %get-tuple-element.48) | copy-start | bytes 196612
  196.1 8.0 %collective-permute-start = (bf16[128,256]{1,0:T(8,128)(2,1)S(1)}, bf16[128,256]{1,0:T(8,128)(2,1)S(1)}, u32[]{:S(2)}, u32[]{:S(2)}) collective-permute-start(bf16[128,256]{1,0:T(8,128)(2,1)S(1)} %get-tuple-element.48), channel_id=1, source_target_pairs={{0,1},{2,3},{4,5},{6,7},{8,9},{10,11},{12,13},{14,15},{16,17},{18,... | collective-permute-start | bytes 196616 | tf_op jit(solution)/shard_map/ppermute | solution.py:18
  201.3 5.8 copy-start
  203.3 0.6 copy-start.35
  204.0 4.0 copy-start.19
  204.0 7.7 %copy-start.26 = (bf16[128,256]{1,0:T(8,128)(2,1)}, bf16[128,256]{1,0:T(8,128)(2,1)S(1)}, u32[]{:S(2)}) copy-start(bf16[128,256]{1,0:T(8,128)(2,1)S(1)} %collective-permute-done) | copy-start | bytes 196612
  204.6 2.7 copy-start.29
  204.6 3.4 copy-start.22
  204.9 2.2 copy-start.13
  205.1 2.0 copy-start.15
  207.3 0.6 copy-start.50
  207.3 0.7 copy-start.43
  211.8 94.6 %copy-start.6 = (f32[1,128,640]{2,1,0:T(8,128)S(1)}, f32[1,128,640]{2,1,0:T(8,128)}, u32[]{:S(2)}) copy-start(f32[1,128,640]{2,1,0:T(8,128)} %param.13) | copy-start | bytes 983044
  211.8 94.6 %copy-start.28 = (f32[640]{0:T(1024)S(1)}, f32[640]{0:T(1024)}, u32[]{:S(2)}) copy-start(f32[640]{0:T(1024)} %get-tuple-element.51) | copy-start | bytes 7684
  308.0 3.3 copy-start.5
  308.0 3.3 copy-start.12
  308.0 3.6 copy-start.21
  316.2 3.5 copy-start.1
  316.2 4.2 copy-start.2
  316.2 4.2 copy-start.44
  319.6 2.0 copy-start.51
  319.6 2.0 copy-start.42
  319.6 2.8 copy-start.49
  319.6 3.0 copy-start.4
  320.4 2.8 copy-start.14
  320.4 3.0 copy-start.30
  320.4 4.0 copy-start.23
  320.4 4.3 copy-start.20
  320.4 5.2 copy-start.25
  320.4 5.2 copy-start.27
  322.5 3.2 copy-start.7
  322.5 6.6 copy-start.34
  326.7 12.6 %copy-start.3 = (bf16[1024,640]{1,0:T(8,128)(2,1)S(1)}, bf16[1024,640]{1,0:T(8,128)(2,1)}, u32[]{:S(2)}) copy-start(bf16[1024,640]{1,0:T(8,128)(2,1)} %all-gather.6.cloned.1.call-done) | copy-start | bytes 3932164
  329.1 13.1 %copy-start.32 = (f32[256]{0:T(256)S(1)}, f32[256]{0:T(256)}, u32[]{:S(2)}) copy-start(f32[256]{0:T(256)} %copy-done.31) | copy-start | bytes 3076
  329.1 15.8 %copy-start.10 = (bf16[256,640]{1,0:T(8,128)(2,1)S(1)}, bf16[256,640]{1,0:T(8,128)(2,1)}, u32[]{:S(2)}) copy-start(bf16[256,640]{1,0:T(8,128)(2,1)} %copy-done.9) | copy-start | bytes 983044
  331.7 16.2 %copy-start.37 = (f32[640]{0:T(1024)S(1)}, f32[640]{0:T(1024)}, u32[]{:S(2)}) copy-start(f32[640]{0:T(1024)} %get-tuple-element.16) | copy-start | bytes 7684
  331.8 17.5 %copy-start.36 = (f32[640]{0:T(1024)S(1)}, f32[640]{0:T(1024)}, u32[]{:S(2)}) copy-start(f32[640]{0:T(1024)} %get-tuple-element.14) | copy-start | bytes 7684
  331.9 7.4 copy-start.16
  333.0 7.8 %collective-permute-start.2 = (bf16[128,256]{1,0:T(8,128)(2,1)S(1)}, bf16[128,256]{1,0:T(8,128)(2,1)S(1)}, u32[]{:S(2)}, u32[]{:S(2)}) collective-permute-start(bf16[128,256]{1,0:T(8,128)(2,1)S(1)} %slice.132), channel_id=1, source_target_pairs={{1,0},{3,2},{5,4},{7,6},{9,8},{11,10},{13,12},{15,14},{17,16},{19,... | collective-permute-start | bytes 196616 | tf_op jit(solution)/shard_map/ppermute | solution.py:18
  335.8 9.4 %collective-permute-start.3 = (bf16[128,256]{0,1:T(8,128)(2,1)}, bf16[128,256]{0,1:T(8,128)(2,1)}, u32[]{:S(2)}, u32[]{:S(2)}) collective-permute-start(bf16[128,256]{0,1:T(8,128)(2,1)} %slice.131), channel_id=1, source_target_pairs={{1,0},{3,2},{5,4},{7,6},{9,8},{11,10},{13,12},{15,14},{17,16},{19,... | collective-permute-start | bytes 196616 | tf_op jit(solution)/shard_map/ppermute | solution.py:18
  339.3 27.9 %slice-start.2 = ((s8[5242880]{0:T(1024)(128)(4,1)}), s8[1048576]{0:T(1024)(128)(4,1)S(1)}, s32[]{:S(2)}) async-start(s8[5242880]{0:T(1024)(128)(4,1)} %bitcast.171), calls=%async_computation.8 | async-start | bytes 2097152
  358.5 8.8 %slice-start.3 = ((s8[5242880]{0:T(1024)(128)(4,1)}), s8[4194304]{0:T(1024)(128)(4,1)S(1)}, s32[]{:S(2)}) async-start(s8[5242880]{0:T(1024)(128)(4,1)} %bitcast.171), calls=%async_computation.9 | async-start | bytes 8388608
  361.6 8.4 %slice-start = ((s8[5242880]{0:T(1024)(128)(4,1)}), s8[4194304]{0:T(1024)(128)(4,1)S(1)}, s32[]{:S(2)}) async-start(s8[5242880]{0:T(1024)(128)(4,1)} %bitcast.168), calls=%async_computation.6 | async-start | bytes 8388608
  367.3 2.7 slice-start.1
  399.4 0.6 copy-start.46
  399.4 1.0 copy-start.8
  399.4 1.0 copy-start.39
  (2 other events, 1.1 us)
Sparse Core Ops, SparseCore 0:
  10.8 57.3 all-gather.5
  71.0 53.6 all-gather.7
  127.6 57.5 all-gather.9
  188.0 56.5 all-gather.11
  247.3 56.5 all-gather.13
  399.6 358.2 all-reduce.8
where the time goes:
time: 772 us; the launch traced here: 771 us
  waiting for transfers between devices  447 us (58%)
  blocking collectives  177 us (23%)
  local copies, waits for them, and re-layouts  61.6 us (8%)
  matrix products  45.6 us (6%)
  other arithmetic  15.8 us (2%)
  between operations  15.1 us (2%)
  starting transfers between devices  8.51 us (1%)
    unnamed x7, waiting for transfers between devices  359 us
    all_gather x1, blocking collectives, on_device(): lax.all_gather(shards[2], ('dp', 'seq'), axis=0, tiled=True)  68.4 us
    all_gather x1, blocking collectives, on_device(): lax.all_gather(shards[1], ('dp', 'seq'), axis=0, tiled=True)  66.4 us
    all_gather x1, waiting for transfers between devices, on_device(): lax.all_gather(shards[6], ('dp', 'seq'), axis=0, tiled=True)  55.4 us
    unnamed x1, blocking collectives  42.1 us
    all_gather x1, waiting for transfers between devices, on_device(): lax.all_gather(shards[5], ('dp', 'seq'), axis=0, tiled=True)  32.8 us
    reshape x1, local copies, waits for them, and re-layouts, packed_term(): return jnp.concatenate(blocks, axis=1).reshape(groups * per_device, D)  23.7 us
    unnamed x122, local copies, waits for them, and re-layouts  21.5 us
  transfers between devices with their start and end apart: 10, of which 3 were waited for; matrix products, arithmetic and copies ran while one was open for 4% of the time, Pallas kernels for 0%

commit v1 on v0

--- a/solution.py
+++ b/solution.py
@@ -1,6 +1,10 @@
+import functools
+
 import jax
 import jax.numpy as jnp
 from jax import lax
+from jax.experimental import pallas as pl
+from jax.experimental.pallas import tpu as pltpu
 from jax.sharding import PartitionSpec as P
 
 D = 640
@@ -81,24 +85,260 @@
     return jnp.where(allowed[None], by_head, -1e30).reshape(raw_scores.shape)
 
 
-def packed_term(entries, gain_terms, gain_share, per_device, count):
-    groups = count // per_device
-    blocks = []
-    for left, right, width in entries:
-        blocks.append(outer_sum(left, right).reshape(groups, width, D))
-    portion = gain_terms
-    portion = jnp.pad(portion.reshape(groups, 1, gain_share), ((0, 0), (0, 0), (0, D - gain_share)))
-    blocks.append(portion)
-    return jnp.concatenate(blocks, axis=1).reshape(groups * per_device, D)
-
-
-def unpack_rows(summed, widths):
-    pieces = []
-    offset = 0
-    for width in widths:
-        pieces.append(summed[offset : offset + width])
-        offset = offset + width
-    return pieces
+MESH_ID = pl.DeviceIdType.MESH
+AXIS_Z, AXIS_Y, AXIS_CORE, AXIS_X = range(4)
+GATHER_ORDERS = (
+    (AXIS_Z, AXIS_Y, AXIS_X, AXIS_CORE),
+    (AXIS_Z, AXIS_X, AXIS_Y, AXIS_CORE),
+)
+SCATTER_ORDERS = (
+    (AXIS_CORE, AXIS_X, AXIS_Y, AXIS_Z),
+    (AXIS_CORE, AXIS_Y, AXIS_X, AXIS_Z),
+)
+
+
+def grid_sizes(dp_size, seq_size):
+    return (dp_size // 4, 2, 2, seq_size)
+
+
+def own_place():
+    dp_index = lax.axis_index("dp")
+    return (dp_index // 4, (dp_index // 2) % 2, dp_index % 2, lax.axis_index("seq"))
+
+
+def peer_place(place, axis, size, hop):
+    moved = list(place)
+    moved[axis] = (place[axis] + hop) % size
+    return tuple(moved)
+
+
+def device_of(place):
+    return ((place[AXIS_Z] * 2 + place[AXIS_Y]) * 2 + place[AXIS_CORE], place[AXIS_X])
+
+
+def greet(place, sizes):
+    barrier = pltpu.get_barrier_semaphore()
+    count = 0
+    for axis, size in enumerate(sizes):
+        for hop in range(1, size):
+            pl.semaphore_signal(
+                barrier,
+                inc=1,
+                device_id=device_of(peer_place(place, axis, size, hop)),
+                device_id_type=MESH_ID,
+            )
+            count += 1
+    pl.semaphore_wait(barrier, count)
+
+
+def slot_table(order, sizes):
+    slots = {}
+    for axis in order:
+        for hop in range(1, sizes[axis]):
+            slots[(axis, hop)] = len(slots)
+    return slots
+
+
+def gather_kernel(sizes, orders, *refs):
+    count = len(orders)
+    shards, wholes = refs[:count], refs[count : 2 * count]
+    local_sem, send_sem, recv_sem = refs[2 * count :]
+    place = own_place()
+    tables = [slot_table(order, sizes) for order in orders]
+
+    def block(ref, held):
+        return ref.at[tuple(slice(None) if a in held else place[a] for a in range(4))]
+
+    def start(i, stage):
+        axis = orders[i][stage]
+        held = orders[i][:stage]
+        copies = []
+        for hop in range(1, sizes[axis]):
+            slot = tables[i][(axis, hop)]
+            copies.append(
+                pltpu.make_async_remote_copy(
+                    src_ref=block(wholes[i], held) if stage else shards[i],
+                    dst_ref=block(wholes[i], held),
+                    send_sem=send_sem.at[i, slot],
+                    recv_sem=recv_sem.at[i, slot],
+                    device_id=device_of(peer_place(place, axis, sizes[axis], hop)),
+                    device_id_type=MESH_ID,
+                )
+            )
+        for copy in copies:
+            copy.start()
+        return copies
+
+    own = [
+        pltpu.make_async_copy(shards[i], block(wholes[i], ()), local_sem.at[i])
+        for i in range(count)
+    ]
+    for copy in own:
+        copy.start()
+    greet(place, sizes)
+    flying = [[start(i, 0)] for i in range(count)]
+    for tick in range(count + 3):
+        for stage in range(4):
+            i = tick - stage
+            if not 0 <= i < count:
+                continue
+            if stage == 0:
+                own[i].wait()
+            for copy in flying[i][stage]:
+                copy.wait()
+            if stage < 3:
+                flying[i].append(start(i, stage + 1))
+
+
+def gather_all(sizes, orders, shards):
+    count = len(shards)
+    slots = sum(size - 1 for size in sizes)
+    return pl.pallas_call(
+        functools.partial(gather_kernel, sizes, orders),
+        out_shape=[jax.ShapeDtypeStruct(sizes + s.shape, s.dtype) for s in shards],
+        in_specs=[pl.BlockSpec(memory_space=pl.ANY)] * count,
+        out_specs=[pl.BlockSpec(memory_space=pl.ANY)] * count,
+        scratch_shapes=[
+            pltpu.SemaphoreType.DMA((count,)),
+            pltpu.SemaphoreType.DMA((count, slots)),
+            pltpu.SemaphoreType.DMA((count, slots)),
+        ],
+        compiler_params=pltpu.CompilerParams(collective_id=0, has_side_effects=True),
+        name="gather_all",
+    )(*shards)
+
+
+def scatter_kernel(sizes, orders, *refs):
+    count = len(orders)
+    terms, outs = refs[:count], refs[count : 2 * count]
+    buffers = refs[2 * count : 9 * count]
+    local_sem, send_sem, recv_sem = refs[9 * count :]
+    place = own_place()
+    tables = [slot_table(order, sizes) for order in orders]
+    partial = [list(buffers[7 * i : 7 * i + 3]) for i in range(count)]
+    landing = [list(buffers[7 * i + 3 : 7 * i + 7]) for i in range(count)]
+
+    def pick(ref, axes, axis, index):
+        return ref.at[tuple(index if a == axis else slice(None) for a in axes)]
+
+    def remaining(i, stage):
+        return [a for a in range(4) if a not in orders[i][:stage]]
+
+    def source(i, stage):
+        return partial[i][stage - 1] if stage else terms[i]
+
+    def start(i, stage):
+        axis = orders[i][stage]
+        axes = remaining(i, stage)
+        copies = []
+        for hop in range(1, sizes[axis]):
+            slot = tables[i][(axis, hop)]
+            peer = peer_place(place, axis, sizes[axis], hop)
+            copies.append(
+                pltpu.make_async_remote_copy(
+                    src_ref=pick(source(i, stage), axes, axis, peer[axis]),
+                    dst_ref=landing[i][stage].at[hop - 1],
+                    send_sem=send_sem.at[i, slot],
+                    recv_sem=recv_sem.at[i, slot],
+                    device_id=device_of(peer),
+                    device_id_type=MESH_ID,
+                )
+            )
+        for copy in copies:
+            copy.start()
+        return copies
+
+    def reduce(i, stage):
+        axis = orders[i][stage]
+        axes = remaining(i, stage)
+        rest = [a for a in axes if a != axis]
+        target = partial[i][stage] if stage < 3 else outs[i]
+        steps = 1
+        for a in rest:
+            steps *= sizes[a]
+
+        def body(step, carry):
+            index = []
+            left = step
+            for a in reversed(rest):
+                index.insert(0, left % sizes[a])
+                left = left // sizes[a]
+            by_axis = dict(zip(rest, index))
+            if stage:
+                mine = source(i, stage)[
+                    tuple(place[axis] if a == axis else by_axis[a] for a in axes)
+                ]
+            else:
+                mine = target[tuple(index)]
+            total = mine.astype(jnp.float32)
+            for hop in range(1, sizes[axis]):
+                total += landing[i][stage][(hop - 1, *index)].astype(jnp.float32)
+            if stage < 3:
+                target[tuple(index)] = total.astype(target.dtype)
+            else:
+                target[...] = total
+            return carry
+
+        if steps == 1:
+            body(0, 0)
+        else:
+            lax.fori_loop(0, steps, body, 0)
+
+    own = [
+        pltpu.make_async_copy(
+            pick(terms[i], range(4), orders[i][0], place[orders[i][0]]),
+            partial[i][0],
+            local_sem.at[i],
+        )
+        for i in range(count)
+    ]
+    for copy in own:
+        copy.start()
+    greet(place, sizes)
+    flying = [[start(i, 0)] for i in range(count)]
+    for tick in range(count + 3):
+        for stage in range(4):
+            i = tick - stage
+            if not 0 <= i < count:
+                continue
+            if stage == 0:
+                own[i].wait()
+            for copy in flying[i][stage]:
+                copy.wait()
+            reduce(i, stage)
+            if stage < 3:
+                flying[i].append(start(i, stage + 1))
+
+
+def scatter_sum(sizes, orders, terms):
+    count = len(terms)
+    slots = sum(size - 1 for size in sizes)
+    buffers = []
+    for order, term in zip(orders, terms):
+        tile = term.shape[4:]
+        partial, landing = [], []
+        for stage, axis in enumerate(order):
+            rest = tuple(sizes[a] for a in range(4) if a not in order[: stage + 1])
+            if stage < 3:
+                partial.append(pltpu.VMEM(rest + tile, term.dtype))
+            landing.append(pltpu.VMEM((max(sizes[axis] - 1, 1),) + rest + tile, term.dtype))
+        buffers.extend(partial + landing)
+    return pl.pallas_call(
+        functools.partial(scatter_kernel, sizes, orders),
+        out_shape=[jax.ShapeDtypeStruct(t.shape[4:], jnp.float32) for t in terms],
+        in_specs=[pl.BlockSpec(memory_space=pl.ANY)] * count,
+        out_specs=[pl.BlockSpec(memory_space=pltpu.VMEM)] * count,
+        scratch_shapes=buffers
+        + [
+            pltpu.SemaphoreType.DMA((count,)),
+            pltpu.SemaphoreType.DMA((count, slots)),
+            pltpu.SemaphoreType.DMA((count, slots)),
+        ],
+        compiler_params=pltpu.CompilerParams(
+            collective_id=1, has_side_effects=True, vmem_limit_bytes=44 * 1024 * 1024
+        ),
+        name="scatter_sum",
+    )(*terms)
 
 
 def on_device(
@@ -117,33 +357,35 @@
     tokens_here = inputs.shape[1]
     scale = HD ** (-0.5)
     block_index = lax.axis_index("seq")
-    shards = (
-        q_weight,
-        k_weight,
-        v_weight,
-        o_weight,
-        gate_weight,
-        up_weight,
-        down_weight,
-        norm_gains,
-    )
+    sizes = grid_sizes(lax.axis_size("dp"), lax.axis_size("seq"))
+    devices = lax.axis_size(("dp", "seq"))
     width_query = q_weight.shape[0]
     width_key = k_weight.shape[0]
     width_ffn = gate_weight.shape[0]
     gain_share = norm_gains.shape[0]
-    gathered = (
-        lax.all_gather(shards[0], ("dp", "seq"), axis=0, tiled=True),
-        lax.all_gather(shards[1], ("dp", "seq"), axis=0, tiled=True),
-        lax.all_gather(shards[2], ("dp", "seq"), axis=0, tiled=True),
-        lax.all_gather(shards[3], ("dp", "seq"), axis=0, tiled=True),
-        lax.all_gather(shards[4], ("dp", "seq"), axis=0, tiled=True),
-        lax.all_gather(shards[5], ("dp", "seq"), axis=0, tiled=True),
-        lax.all_gather(shards[6], ("dp", "seq"), axis=0, tiled=True),
-        lax.all_gather(shards[7], ("dp", "seq"), axis=0, tiled=True),
-    )
-    w_query, w_key, w_value, w_out, w_gate, w_upper, w_down = gathered[:7]
+    gain_tile = jnp.pad(norm_gains[None], ((0, 15), (0, -gain_share % 128)))
+    first, second = GATHER_ORDERS
+    all_gains, w_query, w_kv, w_out, w_upper, w_gate, w_down = gather_all(
+        sizes,
+        (second, first, second, first, second, first, second),
+        (
+            gain_tile,
+            q_weight,
+            jnp.concatenate([k_weight, v_weight], axis=0),
+            o_weight,
+            up_weight,
+            gate_weight,
+            down_weight,
+        ),
+    )
+    w_query, w_out, w_upper, w_gate, w_down = [
+        w.reshape(-1, D) for w in (w_query, w_out, w_upper, w_gate, w_down)
+    ]
+    w_kv = w_kv.reshape(devices, 2 * width_key, D)
+    w_key = w_kv[:, :width_key].reshape(-1, D)
+    w_value = w_kv[:, width_key:].reshape(-1, D)
     gain_in, gain_attn, gain_pre, gain_post, gain_query, gain_key = split_gains(
-        gathered[7].astype(jnp.float32)
+        all_gains.reshape(devices, 16, -1)[:, 0, :gain_share].reshape(-1).astype(jnp.float32)
     )
     seq_inputs = inputs[0]
     seq_cotangent = cotangent[0]
@@ -184,20 +426,6 @@
     hidden = glu_product(gate_pre, up_pre).astype(jnp.bfloat16)
     ffn_out = times_plain(hidden, w_down)
     output = middle + rms_scale(ffn_out, gain_post)
-    regathered = (
-        lax.all_gather(shards[0], ("dp", "seq"), axis=0, tiled=True),
-        lax.all_gather(shards[1], ("dp", "seq"), axis=0, tiled=True),
-        lax.all_gather(shards[2], ("dp", "seq"), axis=0, tiled=True),
-        lax.all_gather(shards[3], ("dp", "seq"), axis=0, tiled=True),
-        lax.all_gather(shards[4], ("dp", "seq"), axis=0, tiled=True),
-        lax.all_gather(shards[5], ("dp", "seq"), axis=0, tiled=True),
-        lax.all_gather(shards[6], ("dp", "seq"), axis=0, tiled=True),
-        lax.all_gather(shards[7], ("dp", "seq"), axis=0, tiled=True),
-    )
-    w_query, w_key, w_value, w_out, w_gate, w_upper, w_down = regathered[:7]
-    gain_in, gain_attn, gain_pre, gain_post, gain_query, gain_key = split_gains(
-        regathered[7].astype(jnp.float32)
-    )
     unused, pull = jax.vjp(rms_scale, ffn_out, gain_post)
     d_ffn, grad_post = pull(seq_cotangent)
     d_ffn = d_ffn.astype(jnp.bfloat16)
@@ -207,11 +435,6 @@
     d_gate = d_gate.astype(jnp.bfloat16)
     d_up = d_up.astype(jnp.bfloat16)
     d_normed_ff = times_plain(d_gate, w_gate) + times_plain(d_up, w_upper)
-    ffn_entries = [
-        (d_gate, normed_ff, width_ffn),
-        (d_up, normed_ff, width_ffn),
-        (hidden, d_ffn, width_ffn),
-    ]
     unused, pull = jax.vjp(rms_scale, middle, gain_pre)
     d_mid_norm, grad_pre = pull(d_normed_ff)
     d_middle = seq_cotangent + d_mid_norm
@@ -258,28 +481,47 @@
     d_in_norm, grad_in = pull(d_normed_in)
     input_grad = d_middle + d_in_norm
     gains_grad = jnp.concatenate([grad_in, grad_attn, grad_pre, grad_post, grad_query, grad_key])
-    attn_entries = [
-        (d_queries, normed_in, width_query),
-        (d_keys, normed_in, width_key),
-        (d_values, normed_in, width_key),
-        (merged, d_branch, width_query),
-    ]
-    attn_widths = [width_query, width_key, width_key, width_query]
-    all_rows = 2 * width_query + 2 * width_key + 3 * width_ffn + 1
-    summed = lax.psum_scatter(
-        packed_term(
-            attn_entries + ffn_entries,
-            gains_grad,
-            gain_share,
-            all_rows,
-            lax.axis_size(("dp", "seq")) * all_rows,
+
+    def grad_term(left, right):
+        return outer_sum(left, right).astype(jnp.bfloat16)
+
+    def by_owner(term):
+        return term.reshape(sizes + (-1, term.shape[-1]))
+
+    kv_term = jnp.concatenate(
+        [
+            grad_term(d_keys, normed_in).reshape(devices, width_key, D),
+            grad_term(d_values, normed_in).reshape(devices, width_key, D),
+        ],
+        axis=1,
+    )
+    gain_term = jnp.pad(
+        gains_grad.reshape(devices, 1, gain_share), ((0, 0), (0, 7), (0, -gain_share % 128))
+    )
+    first, second = SCATTER_ORDERS
+    gains_sum, down_sum, gate_sum, up_sum, o_sum, q_sum, kv_sum = scatter_sum(
+        sizes,
+        (second, first, second, first, second, first, second),
+        (
+            gain_term.reshape(sizes + gain_term.shape[1:]),
+            by_owner(grad_term(hidden, d_ffn)),
+            by_owner(grad_term(d_gate, normed_ff)),
+            by_owner(grad_term(d_up, normed_ff)),
+            by_owner(grad_term(merged, d_branch)),
+            by_owner(grad_term(d_queries, normed_in)),
+            kv_term.reshape(sizes + kv_term.shape[1:]),
         ),
-        ("dp", "seq"),
-        scatter_dimension=0,
-        tiled=True,
-    )
-    parts = unpack_rows(summed, attn_widths + [width_ffn, width_ffn, width_ffn, 1])
-    results = tuple(parts[:7]) + (parts[7][0, :gain_share],)
+    )
+    results = (
+        q_sum,
+        kv_sum[:width_key],
+        kv_sum[width_key:],
+        o_sum,
+        gate_sum,
+        up_sum,
+        down_sum,
+        gains_sum[0, :gain_share],
+    )
     return (output[None], input_grad[None]) + results
 
 

time: 772 us -> 238 us (0.31)
  waiting for transfers between devices: 447 us -> 3.93 us
  blocking collectives: 177 us -> 0 us
  Pallas kernels: 0 us -> 146 us
  local copies, waits for them, and re-layouts: 61.6 us -> 27.2 us
  between operations: 15.1 us -> 1.62 us
  matrix products: 45.6 us -> 33.3 us
    unnamed x7 -> x0, waiting for transfers between devices: 359 us -> none
    pallas_call x0 -> x2, Pallas kernels: none -> 146 us  [the longest x1 74.1 us: scatter_sum(): pl.pallas_call(functools.partial(scatter_kernel, sizes, orders), out_shap...]
    all_gather x2 -> x0, blocking collectives: 135 us -> none  [the longest x1 68.4 us: on_device(): lax.all_gather(shards[2], ('dp', 'seq'), axis=0, tiled=True)]
    all_gather x5 -> x0, waiting for transfers between devices: 88.2 us -> none  [the longest x1 55.4 us: on_device(): lax.all_gather(shards[6], ('dp', 'seq'), axis=0, tiled=True)]
    unnamed x1 -> x0, blocking collectives: 42.1 us -> none
    reshape x2 -> x1, local copies, waits for them, and re-layouts: 24.5 us -> 0.8 us  [on_device(): gains_grad.reshape(devices, 1, gain_share)]
    unnamed x122 -> x128, local copies, waits for them, and re-layouts: 21.5 us -> 16.2 us
  transfers between devices with their start and end apart: 10 -> 4, of which waited for: 3 -> 2; matrix products, arithmetic and copies ran while one was open for 4% -> 3% of each run, Pallas kernels for 0% -> 0%
where the time goes in v1:
time: 238 us; the launch traced here: 236 us
  Pallas kernels  146 us (61%)
  matrix products  33.3 us (14%)
  local copies, waits for them, and re-layouts  27.2 us (11%)
  other arithmetic  15.7 us (7%)
  starting transfers between devices  8.84 us (4%)
  waiting for transfers between devices  3.93 us (2%)
    pallas_call x1, Pallas kernels, scatter_sum(): pl.pallas_call(functools.partial(scatter_kernel, sizes, orders), out_shap...  74.1 us
    pallas_call x1, Pallas kernels, gather_all(): pl.pallas_call(functools.partial(gather_kernel, sizes, orders), out_shape...  71.8 us
    unnamed x128, local copies, waits for them, and re-layouts  16.2 us
    dot_general x9, matrix products, outer_sum(): lax.dot_general(left, right, (((0,), (0,)), ((), ())), preferred_element_...  13.4 us
    dot_general x9, matrix products, times_plain(): return jnp.dot(left, weight, preferred_element_type=jnp.float32)  10.8 us
    dot_general x9, matrix products, times_rows(): lax.dot_general(left, weight, (((1,), (1,)), ((), ())), preferred_element...  9.13 us
    ppermute x4, starting transfers between devices, shifted(): return lax.ppermute(block, axis, route)  8.84 us
  transfers between devices with their start and end apart: 4, of which 2 were waited for; matrix products, arithmetic and copies ran while one was open for 3% of the time, Pallas kernels for 0%

profile of v1, /device:TPU:0, one launch (start us, length us, event | category | flops | bytes accessed | tf_op | source)
XLA Modules:
  0.0 236.4 jit_solution(9284026741796631547)
XLA Ops:
  0.7 1.3 pad.20.refs_0_
  1.9 1.3 pad_maximum_fusion.8.refs_2_
  3.2 71.8 %gather_all.1 = (bf16[4,2,2,2,16,128]{5,4,3,2,1,0:T(8,128)(2,1)}, bf16[4,2,2,2,32,640]{5,4,3,2,1,0:T(8,128)(2,1)}, bf16[4,2,2,2,16,640]{5,4,3,2,1,0:T(8,128)(2,1...) custom-call(bf16[16,128]{1,0:T(8,128)(2,1)} %pad.20.refs_0_, ...), custom_call_target="tpu_custom_call" | custom-call | tf_op jit(solution)/shard_map/gather_all/pallas_call | solution.py:196
  75.0 1.0 fusion.49
  76.1 0.6 fusion.67
  76.7 1.1 fusion.21
  77.8 1.1 multiply_convert_fusion.4
  78.9 1.9 convolution_convert_fusion.9
  80.8 4.8 %collective-permute-start.1 = (bf16[128,256]{1,0:T(8,128)(2,1)}, bf16[128,256]{1,0:T(8,128)(2,1)}, u32[]{:S(2)}, u32[]{:S(2)}) collective-permute-start(bf16[128,256]{1,0:T(8,128)(2,1)} %convolution_convert_fusion.9), channel_id=1, source_target_pairs={{0,1},{2,3},{4,5},{6,7},{8,9},{10,11},{12,13},{14,15},{16,17},{18,... | collective-permute-start | bytes 196616 | tf_op jit(solution)/shard_map/ppermute | solution.py:22
  85.7 1.3 multiply_reduce_fusion.13
  88.1 1.3 collective-permute-start
  89.4 0.6 multiply_reduce_fusion.3
  92.5 2.1 convolution_convert_fusion.8
  94.6 1.8 copy.25
  96.4 1.9 multiply_reduce_fusion.12
  98.7 1.0 fusion.70
  100.0 1.0 multiply_convert_fusion.1
  101.1 0.7 copy-done.21
  101.8 0.7 multiply_reduce_fusion.10
  102.5 0.7 fusion.20
  103.2 0.9 fusion.15
  104.1 0.9 convolution_convert_fusion.2
  105.0 1.4 multiply_convert_fusion
  106.7 0.6 fusion.71
  107.3 2.4 %convolution_convert_fusion.1 = bf16[2048,640]{1,0:T(8,128)(2,1)} fusion(bf16[128,2048]{1,0:T(8,128)(2,1)S(1)} %get-tuple-element.58, bf16[128,640]{1,0:T(8,128)(2,1)S(1)} %multiply_convert_fusion.3), kind=kOutput, calls=%fused_computation.1 | convolution fusion | flops 336855040 | bytes 3309568 | tf_op jit(solution)/shard_map/dot_general | solution.py:77
  109.7 2.4 %convolution_convert_fusion = bf16[2048,640]{1,0:T(8,128)(2,1)} fusion(bf16[128,2048]{1,0:T(8,128)(2,1)S(1)} %get-tuple-element.57, bf16[128,640]{1,0:T(8,128)(2,1)S(1)} %multiply_convert_fusion.3), kind=kOutput, calls=%fused_computation | convolution fusion | flops 336855040 | bytes 3309568 | tf_op jit(solution)/shard_map/dot_general | solution.py:77
  112.1 1.2 multiply_reduce_fusion.4
  113.3 0.8 multiply_reduce_fusion.5
  114.2 0.7 copy-done.19
  115.6 1.6 convolution_convert_fusion.4
  117.4 1.1 fusion.2
  118.6 0.9 convolution_multiply_fusion.2
  119.6 1.1 convolution_multiply_fusion
  120.6 2.0 copy.29
  122.7 1.2 multiply_bitcast_fusion
  123.9 1.9 multiply_reduce_fusion
  125.8 0.9 fusion.10
  126.7 1.8 copy.30
  128.6 2.6 %convolution_convert_fusion.3 = bf16[1024,640]{1,0:T(8,128)(2,1)} fusion(bf16[128,1024]{0,1:T(8,128)(2,1)} %bitcast.201, bf16[1,128,640]{2,1,0:T(8,128)(2,1)} %copy-done.14), kind=kOutput, calls=%fused_computation.3 | convolution fusion | flops 168427520 | bytes 1736704 | tf_op jit(solution)/shard_map/dot_general | solution.py:77
  131.2 2.1 fusion.72
  133.3 1.3 collective-permute-start.2
  134.9 1.4 collective-permute-start.3
  136.3 3.4 %collective-permute-done.2 = bf16[128,256]{1,0:T(8,128)(2,1)S(1)} collective-permute-done((bf16[128,256]{1,0:T(8,128)(2,1)S(1)}, bf16[128,256]{1,0:T(8,128)(2,1)S(1)}, u32[]{:S(2)}, u32[]{:S(2)}) %collective-permute-start.2) | collective-permute-done | bytes 65568 | tf_op jit(solution)/shard_map/ppermute | solution.py:22
  140.9 1.0 convolution_convert_fusion.6
  141.9 1.0 multiply_reduce_fusion.6
  143.0 1.3 constant_dynamic-update-slice_fusion.5
  144.3 1.3 constant_dynamic-update-slice_fusion.4
  145.6 1.3 constant_dynamic-update-slice_fusion.3
  146.9 1.3 constant_dynamic-update-slice_fusion.2
  148.2 1.3 constant_dynamic-update-slice_fusion.1
  149.5 1.3 constant_dynamic-update-slice_fusion
  150.8 0.8 reshape.503
  151.6 1.3 convolution_convert_fusion.5
  152.9 1.0 pad_maximum_fusion.refs_6_
  154.0 1.7 copy-done
  155.7 1.3 copy-done.2
  157.0 74.1 %scatter_sum.1 = (f32[8,128]{1,0:T(8,128)S(1)}, f32[64,640]{1,0:T(8,128)S(1)}, f32[64,640]{1,0:T(8,128)S(1)}, f32[64,640]{1,0:T(8,128)S(1)}, f32[32,640]{1,0:T(8...) custom-call(f32[4,2,2,2,8,128]{5,4,3,2,1,0:T(8,128)S(1)} %bitcast.182, ...), custom_call_target="tpu_custom_call" | custom-call | tf_op jit(solution)/shard_map/scatter_sum/pallas_call | solution.py:326
  231.2 0.6 fusion.66
  232.3 0.9 fusion.19
  233.1 0.6 copy.49
  233.8 0.6 copy.50
  234.4 0.7 copy.51
  235.1 0.7 copy.52
  235.7 0.7 copy.53
  (166 shorter events, 7.5 us)
Async XLA Ops:
  0.6 86.5 %copy-start.54 = (s32[1,256]{1,0:T(1,128)S(1)}, s32[1,256]{1,0:T(1,128)}, u32[]{:S(2)}) copy-start(s32[1,256]{1,0:T(1,128)} %param.12) | copy-start | bytes 3076
  75.0 14.4 %copy-start.10 = (bf16[4,2,2,2,32,640]{5,4,3,2,1,0:T(8,128)(2,1)S(1)}, bf16[4,2,2,2,32,640]{5,4,3,2,1,0:T(8,128)(2,1)}, u32[]{:S(2)}) copy-start(bf16[4,2,2,2,32,640]{5,4,3,2,1,0:T(8,128)(2,1)} %get-tuple-element.25) | copy-start | bytes 3932164
  77.8 9.4 %copy-start.55 = (f32[128]{0:T(128)}, f32[128]{0:T(128)S(1)}, u32[]{:S(2)}) copy-start(f32[128]{0:T(128)S(1)} %fusion.21) | copy-start | bytes 1540
  77.8 9.4 %copy-start.49 = (f32[128]{0:T(128)}, f32[128]{0:T(128)S(1)}, u32[]{:S(2)}) copy-start(f32[128]{0:T(128)S(1)} %fusion.51) | copy-start | bytes 1540
  78.9 11.3 %copy-start.14 = (bf16[1,128,640]{2,1,0:T(8,128)(2,1)}, bf16[1,128,640]{2,1,0:T(8,128)(2,1)S(1)}, u32[]{:S(2)}) copy-start(bf16[1,128,640]{2,1,0:T(8,128)(2,1)S(1)} %multiply_convert_fusion.4) | copy-start | bytes 491524
  80.8 11.2 %collective-permute-start.1 = (bf16[128,256]{1,0:T(8,128)(2,1)}, bf16[128,256]{1,0:T(8,128)(2,1)}, u32[]{:S(2)}, u32[]{:S(2)}) collective-permute-start(bf16[128,256]{1,0:T(8,128)(2,1)} %convolution_convert_fusion.9), channel_id=1, source_target_pairs={{0,1},{2,3},{4,5},{6,7},{8,9},{10,11},{12,13},{14,15},{16,17},{18,... | collective-permute-start | bytes 196616 | tf_op jit(solution)/shard_map/ppermute | solution.py:22
  85.6 4.6 %copy-start.40 = (f32[256]{0:T(256)}, f32[256]{0:T(256)S(1)}, u32[]{:S(2)}) copy-start(f32[256]{0:T(256)S(1)} %get-tuple-element.78) | copy-start | bytes 3076
  85.6 4.7 %copy-start.42 = (f32[256]{0:T(256)}, f32[256]{0:T(256)S(1)}, u32[]{:S(2)}) copy-start(f32[256]{0:T(256)S(1)} %get-tuple-element.79) | copy-start | bytes 3076
  87.0 0.5 copy-start.57
  87.0 3.3 %copy-start.16 = (f32[128,256]{1,0:T(8,128)}, f32[128,256]{1,0:T(8,128)S(1)}, u32[]{:S(2)}) copy-start(f32[128,256]{1,0:T(8,128)S(1)} %get-tuple-element.84) | copy-start | bytes 393220
  87.0 3.3 %copy-start.51 = (f32[128]{0:T(128)}, f32[128]{0:T(128)S(1)}, u32[]{:S(2)}) copy-start(f32[128]{0:T(128)S(1)} %fusion.52) | copy-start | bytes 1540
  88.1 2.4 %copy-start.28 = (f32[128,256]{1,0:T(8,128)}, f32[128,256]{1,0:T(8,128)S(1)}, u32[]{:S(2)}) copy-start(f32[128,256]{1,0:T(8,128)S(1)} %get-tuple-element.71) | copy-start | bytes 393220
  88.1 2.4 %copy-start.29 = (f32[128,256]{1,0:T(8,128)}, f32[128,256]{1,0:T(8,128)S(1)}, u32[]{:S(2)}) copy-start(f32[128,256]{1,0:T(8,128)S(1)} %get-tuple-element.70) | copy-start | bytes 393220
  88.1 3.3 %copy-start.32 = (bf16[128,256]{1,0:T(8,128)(2,1)}, bf16[128,256]{1,0:T(8,128)(2,1)S(1)}, u32[]{:S(2)}) copy-start(bf16[128,256]{1,0:T(8,128)(2,1)S(1)} %get-tuple-element.69) | copy-start | bytes 196612
  88.1 3.2 %collective-permute-start = (bf16[128,256]{1,0:T(8,128)(2,1)S(1)}, bf16[128,256]{1,0:T(8,128)(2,1)S(1)}, u32[]{:S(2)}, u32[]{:S(2)}) collective-permute-start(bf16[128,256]{1,0:T(8,128)(2,1)S(1)} %get-tuple-element.69), channel_id=1, source_target_pairs={{0,1},{2,3},{4,5},{6,7},{8,9},{10,11},{12,13},{14,15},{16,17},{18,... | collective-permute-start | bytes 196616 | tf_op jit(solution)/shard_map/ppermute | solution.py:22
  90.1 1.4 copy-start.44
  90.5 1.2 copy-start.30
  91.3 0.6 copy-start.35
  91.4 6.9 %copy-start.3 = (f32[1,128,640]{2,1,0:T(8,128)S(1)}, f32[1,128,640]{2,1,0:T(8,128)}, u32[]{:S(2)}) copy-start(f32[1,128,640]{2,1,0:T(8,128)} %param.11) | copy-start | bytes 983044
  91.7 0.8 copy-start.7
  91.9 6.7 %copy-start.5 = (bf16[4,2,2,2,64,640]{5,4,3,2,1,0:T(8,128)(2,1)S(1)}, bf16[4,2,2,2,64,640]{5,4,3,2,1,0:T(8,128)(2,1)}, u32[]{:S(2)}) copy-start(bf16[4,2,2,2,64,640]{5,4,3,2,1,0:T(8,128)(2,1)} %get-tuple-element.28) | copy-start | bytes 7864324
  92.0 2.6 %copy-start.38 = (f32[512]{0:T(512)}, f32[512]{0:T(512)S(1)}, u32[]{:S(2)}) copy-start(f32[512]{0:T(512)S(1)} %log_add_fusion) | copy-start | bytes 6148
  98.3 1.7 copy-start.4
  100.0 1.7 copy-start.21
  101.0 1.4 copy-start.18
  101.0 1.4 copy-start.37
  105.0 1.7 copy-start.6
  112.1 2.9 %copy-start.11 = (bf16[4,2,2,2,32,640]{5,4,3,2,1,0:T(8,128)(2,1)S(1)}, bf16[4,2,2,2,32,640]{5,4,3,2,1,0:T(8,128)(2,1)}, u32[]{:S(2)}) copy-start(bf16[4,2,2,2,32,640]{5,4,3,2,1,0:T(8,128)(2,1)} %get-tuple-element.27) | copy-start | bytes 3932164
  113.3 2.3 copy-start.23
  114.2 0.7 copy-start.19
  114.2 3.1 %copy-start.22 = (bf16[512,256]{1,0:T(8,128)(2,1)S(1)}, bf16[512,256]{1,0:T(8,128)(2,1)}, u32[]{:S(2)}) copy-start(bf16[512,256]{1,0:T(8,128)(2,1)} %convolution_convert_fusion.8) | copy-start | bytes 786436
  114.9 2.6 %copy-start.8 = (f32[512,256]{0,1:T(8,128)S(1)}, f32[512,256]{0,1:T(8,128)}, u32[]{:S(2)}) copy-start(f32[512,256]{0,1:T(8,128)} %copy-done.7) | copy-start | bytes 1572868
  114.9 2.6 %copy-start.39 = (f32[512]{0:T(512)S(1)}, f32[512]{0:T(512)}, u32[]{:S(2)}) copy-start(f32[512]{0:T(512)} %copy-done.38) | copy-start | bytes 6148
  115.0 3.6 %copy-start.31 = (bf16[128,4,256]{2,0,1:T(8,128)(2,1)S(1)}, bf16[128,4,256]{2,0,1:T(8,128)(2,1)}, u32[]{:S(2)}) copy-start(bf16[128,4,256]{2,0,1:T(8,128)(2,1)} %copy-done.30) | copy-start | bytes 786436
  115.6 4.0 %copy-start.33 = (bf16[128,256]{1,0:T(8,128)(2,1)S(1)}, bf16[128,256]{1,0:T(8,128)(2,1)}, u32[]{:S(2)}) copy-start(bf16[128,256]{1,0:T(8,128)(2,1)} %copy-done.32) | copy-start | bytes 196612
  115.6 4.0 %copy-start.36 = (bf16[128,256]{1,0:T(8,128)(2,1)S(1)}, bf16[128,256]{1,0:T(8,128)(2,1)}, u32[]{:S(2)}) copy-start(bf16[128,256]{1,0:T(8,128)(2,1)} %copy-done.35) | copy-start | bytes 196612
  117.2 1.4 copy-start.12
  118.6 5.3 %copy-start.43 = (f32[256]{0:T(256)S(1)}, f32[256]{0:T(256)}, u32[]{:S(2)}) copy-start(f32[256]{0:T(256)} %copy-done.42) | copy-start | bytes 3076
  122.7 3.1 %copy-start.45 = (f32[128,4]{0,1:T(4,128)S(1)}, f32[128,4]{0,1:T(4,128)}, u32[]{:S(2)}) copy-start(f32[128,4]{0,1:T(4,128)} %copy-done.44) | copy-start | bytes 6148
  126.7 7.9 %copy-start.9 = (f32[512,256]{0,1:T(8,128)S(1)}, f32[512,256]{0,1:T(8,128)}, u32[]{:S(2)}) copy-start(f32[512,256]{0,1:T(8,128)} %copy-done.7) | copy-start | bytes 1572868
  128.6 4.7 %copy-start.25 = (f32[256,256]{1,0:T(8,128)S(1)}, f32[256,256]{1,0:T(8,128)}, u32[]{:S(2)}) copy-start(f32[256,256]{1,0:T(8,128)} %convolution_multiply_fusion.2) | copy-start | bytes 786436
  128.6 6.0 %copy-start.13 = (bf16[16,4,8,256]{3,2,0,1:T(8,128)(2,1)S(1)}, bf16[16,4,8,256]{3,2,0,1:T(8,128)(2,1)}, u32[]{:S(2)}) copy-start(bf16[16,4,8,256]{3,2,0,1:T(8,128)(2,1)} %copy-done.12) | copy-start | bytes 786436
  128.6 11.6 %copy-start.17 = (f32[128,256]{1,0:T(8,128)S(1)}, f32[128,256]{1,0:T(8,128)}, u32[]{:S(2)}) copy-start(f32[128,256]{1,0:T(8,128)} %copy-done.16) | copy-start | bytes 393220
  128.6 11.6 %copy-start.41 = (f32[256]{0:T(256)S(1)}, f32[256]{0:T(256)}, u32[]{:S(2)}) copy-start(f32[256]{0:T(256)} %copy-done.40) | copy-start | bytes 3076
  128.6 11.6 %copy-start.52 = (f32[128]{0:T(128)S(1)}, f32[128]{0:T(128)}, u32[]{:S(2)}) copy-start(f32[128]{0:T(128)} %copy-done.51) | copy-start | bytes 1540
  131.2 9.4 %copy-start.58 = (f32[128]{0:T(128)S(1)}, f32[128]{0:T(128)}, u32[]{:S(2)}) copy-start(f32[128]{0:T(128)} %copy-done.57) | copy-start | bytes 1540
  131.2 9.5 %copy-start.24 = (bf16[4,2,2,2,16,640]{5,4,3,2,1,0:T(8,128)(2,1)S(1)}, bf16[4,2,2,2,16,640]{5,4,3,2,1,0:T(8,128)(2,1)}, u32[]{:S(2)}) copy-start(bf16[4,2,2,2,16,640]{5,4,3,2,1,0:T(8,128)(2,1)} %get-tuple-element.26) | copy-start | bytes 1966084
  131.2 9.7 %copy-start.15 = (bf16[1,128,640]{2,1,0:T(8,128)(2,1)S(1)}, bf16[1,128,640]{2,1,0:T(8,128)(2,1)}, u32[]{:S(2)}) copy-start(bf16[1,128,640]{2,1,0:T(8,128)(2,1)} %copy-done.14) | copy-start | bytes 491524
  133.2 8.7 %copy-start.50 = (f32[128]{0:T(128)S(1)}, f32[128]{0:T(128)}, u32[]{:S(2)}) copy-start(f32[128]{0:T(128)} %copy-done.49) | copy-start | bytes 1540
  133.3 6.4 %collective-permute-start.2 = (bf16[128,256]{1,0:T(8,128)(2,1)S(1)}, bf16[128,256]{1,0:T(8,128)(2,1)S(1)}, u32[]{:S(2)}, u32[]{:S(2)}) collective-permute-start(bf16[128,256]{1,0:T(8,128)(2,1)S(1)} %slice.127), channel_id=1, source_target_pairs={{1,0},{3,2},{5,4},{7,6},{9,8},{11,10},{13,12},{15,14},{17,16},{19,... | collective-permute-start | bytes 196616 | tf_op jit(solution)/shard_map/ppermute | solution.py:22
  134.8 8.1 %copy-start.26 = (f32[256,256]{1,0:T(8,128)}, f32[256,256]{1,0:T(8,128)S(1)}, u32[]{:S(2)}) copy-start(f32[256,256]{1,0:T(8,128)S(1)} %fusion.44) | copy-start | bytes 786436
  134.8 8.1 %copy-start.56 = (f32[128]{0:T(128)S(1)}, f32[128]{0:T(128)}, u32[]{:S(2)}) copy-start(f32[128]{0:T(128)} %copy-done.55) | copy-start | bytes 1540
  134.9 9.4 %copy-start.47 = (f32[640]{0:T(1024)S(1)}, f32[640]{0:T(1024)}, u32[]{:S(2)}) copy-start(f32[640]{0:T(1024)} %get-tuple-element.44) | copy-start | bytes 7684
  134.9 10.7 %copy-start.46 = (f32[640]{0:T(1024)S(1)}, f32[640]{0:T(1024)}, u32[]{:S(2)}) copy-start(f32[640]{0:T(1024)} %get-tuple-element.42) | copy-start | bytes 7684
  134.9 12.0 %copy-start.48 = (f32[640]{0:T(1024)S(1)}, f32[640]{0:T(1024)}, u32[]{:S(2)}) copy-start(f32[640]{0:T(1024)} %get-tuple-element.40) | copy-start | bytes 7684
  134.9 13.3 %copy-start.53 = (f32[256]{0:T(256)S(1)}, f32[256]{0:T(256)}, u32[]{:S(2)}) copy-start(f32[256]{0:T(256)} %get-tuple-element.38) | copy-start | bytes 3076
  134.9 7.0 %collective-permute-start.3 = (bf16[128,256]{1,0:T(8,128)(2,1)S(1)}, bf16[128,256]{1,0:T(8,128)(2,1)S(1)}, u32[]{:S(2)}, u32[]{:S(2)}) collective-permute-start(bf16[128,256]{1,0:T(8,128)(2,1)S(1)} %slice.126), channel_id=1, source_target_pairs={{1,0},{3,2},{5,4},{7,6},{9,8},{11,10},{13,12},{15,14},{17,16},{19,... | collective-permute-start | bytes 196616 | tf_op jit(solution)/shard_map/ppermute | solution.py:22
  141.9 1.0 copy-start.34
  151.6 2.4 %copy-start.1 = (bf16[1024,640]{1,0:T(8,128)(2,1)S(1)}, bf16[1024,640]{1,0:T(8,128)(2,1)}, u32[]{:S(2)}) copy-start(bf16[1024,640]{1,0:T(8,128)(2,1)} %convolution_convert_fusion.4) | copy-start | bytes 3932164
  154.0 1.7 copy-start
  155.7 1.3 copy-start.2
  157.0 75.3 %copy-start.20 = (f32[128,640]{1,0:T(8,128)S(1)}, f32[128,640]{1,0:T(8,128)}, u32[]{:S(2)}) copy-start(f32[128,640]{1,0:T(8,128)} %copy-done.19) | copy-start | bytes 983044
  157.0 75.3 %copy-start.27 = (f32[128,640]{1,0:T(8,128)S(1)}, f32[128,640]{1,0:T(8,128)}, u32[]{:S(2)}) copy-start(f32[128,640]{1,0:T(8,128)} %get-tuple-element.94) | copy-start | bytes 983044

commit v2 on v1

--- a/solution.py
+++ b/solution.py
@@ -61,6 +61,15 @@
         gains_all[4 * D : 4 * D + HD],
         gains_all[4 * D + HD : 4 * D + 2 * HD],
     )
+
+
+def lay_end_to_end(parts):
+    whole = sum(part.shape[0] for part in parts)
+    total, before = 0.0, 0
+    for part in parts:
+        total += jnp.pad(part, (before, whole - before - part.shape[0]))
+        before += part.shape[0]
+    return total
 
 
 def times_rows(left, weight):
@@ -139,15 +148,36 @@
     return slots
 
 
-def gather_kernel(sizes, orders, *refs):
-    count = len(orders)
-    shards, wholes = refs[:count], refs[count : 2 * count]
-    local_sem, send_sem, recv_sem = refs[2 * count :]
+PIECE_ROWS = 32
+
+
+def cut_pieces(heights, orders):
+    pieces, rows_given = [], [0] * len(orders)
+    for array, height in enumerate(heights):
+        size = PIECE_ROWS if height % PIECE_ROWS == 0 else height
+        for first in range(0, height, size):
+            which = rows_given.index(min(rows_given))
+            rows_given[which] += size
+            pieces.append((array, first, size, orders[which]))
+    return pieces
+
+
+def rows_of(ref, index, piece):
+    return ref.at[(*index, pl.ds(piece[1], piece[2]))]
+
+
+def gather_kernel(sizes, pieces, arrays, *refs):
+    count = len(pieces)
+    orders = [piece[3] for piece in pieces]
+    shards = [refs[piece[0]] for piece in pieces]
+    wholes = [refs[arrays + piece[0]] for piece in pieces]
+    local_sem, send_sem, recv_sem = refs[2 * arrays :]
     place = own_place()
     tables = [slot_table(order, sizes) for order in orders]
 
-    def block(ref, held):
-        return ref.at[tuple(slice(None) if a in held else place[a] for a in range(4))]
+    def block(i, held):
+        index = tuple(slice(None) if a in held else place[a] for a in range(4))
+        return rows_of(wholes[i], index, pieces[i])
 
     def start(i, stage):
         axis = orders[i][stage]
@@ -157,8 +187,8 @@
             slot = tables[i][(axis, hop)]
             copies.append(
                 pltpu.make_async_remote_copy(
-                    src_ref=block(wholes[i], held) if stage else shards[i],
-                    dst_ref=block(wholes[i], held),
+                    src_ref=block(i, held) if stage else rows_of(shards[i], (), pieces[i]),
+                    dst_ref=block(i, held),
                     send_sem=send_sem.at[i, slot],
                     recv_sem=recv_sem.at[i, slot],
                     device_id=device_of(peer_place(place, axis, sizes[axis], hop)),
@@ -170,7 +200,9 @@
         return copies
 
     own = [
-        pltpu.make_async_copy(shards[i], block(wholes[i], ()), local_sem.at[i])
+        pltpu.make_async_copy(
+            rows_of(shards[i], (), pieces[i]), block(i, ()), local_sem.at[i]
+        )
         for i in range(count)
     ]
     for copy in own:
@@ -190,14 +222,15 @@
                 flying[i].append(start(i, stage + 1))
 
 
-def gather_all(sizes, orders, shards):
-    count = len(shards)
+def gather_all(sizes, shards):
+    pieces = cut_pieces([s.shape[0] for s in shards], GATHER_ORDERS)
+    arrays, count = len(shards), len(pieces)
     slots = sum(size - 1 for size in sizes)
     return pl.pallas_call(
-        functools.partial(gather_kernel, sizes, orders),
+        functools.partial(gather_kernel, sizes, pieces, arrays),
         out_shape=[jax.ShapeDtypeStruct(sizes + s.shape, s.dtype) for s in shards],
-        in_specs=[pl.BlockSpec(memory_space=pl.ANY)] * count,
-        out_specs=[pl.BlockSpec(memory_space=pl.ANY)] * count,
+        in_specs=[pl.BlockSpec(memory_space=pl.ANY)] * arrays,
+        out_specs=[pl.BlockSpec(memory_space=pl.ANY)] * arrays,
         scratch_shapes=[
             pltpu.SemaphoreType.DMA((count,)),
             pltpu.SemaphoreType.DMA((count, slots)),
@@ -208,24 +241,26 @@
     )(*shards)
 
 
-def scatter_kernel(sizes, orders, *refs):
-    count = len(orders)
-    terms, outs = refs[:count], refs[count : 2 * count]
-    buffers = refs[2 * count : 9 * count]
-    local_sem, send_sem, recv_sem = refs[9 * count :]
+def scatter_kernel(sizes, pieces, arrays, *refs):
+    count = len(pieces)
+    orders = [piece[3] for piece in pieces]
+    terms = [refs[piece[0]] for piece in pieces]
+    outs = [rows_of(refs[arrays + piece[0]], (), piece) for piece in pieces]
+    buffers = refs[2 * arrays : 2 * arrays + 7 * count]
+    local_sem, send_sem, recv_sem = refs[2 * arrays + 7 * count :]
     place = own_place()
     tables = [slot_table(order, sizes) for order in orders]
     partial = [list(buffers[7 * i : 7 * i + 3]) for i in range(count)]
     landing = [list(buffers[7 * i + 3 : 7 * i + 7]) for i in range(count)]
 
-    def pick(ref, axes, axis, index):
-        return ref.at[tuple(index if a == axis else slice(None) for a in axes)]
+    def pick(i, stage, axes, axis, index):
+        where = tuple(index if a == axis else slice(None) for a in axes)
+        if stage:
+            return partial[i][stage - 1].at[where]
+        return rows_of(terms[i], where, pieces[i])
 
     def remaining(i, stage):
         return [a for a in range(4) if a not in orders[i][:stage]]
-
-    def source(i, stage):
-        return partial[i][stage - 1] if stage else terms[i]
 
     def start(i, stage):
         axis = orders[i][stage]
@@ -236,7 +271,7 @@
             peer = peer_place(place, axis, sizes[axis], hop)
             copies.append(
                 pltpu.make_async_remote_copy(
-                    src_ref=pick(source(i, stage), axes, axis, peer[axis]),
+                    src_ref=pick(i, stage, axes, axis, peer[axis]),
                     dst_ref=landing[i][stage].at[hop - 1],
                     send_sem=send_sem.at[i, slot],
                     recv_sem=recv_sem.at[i, slot],
@@ -265,7 +300,7 @@
                 left = left // sizes[a]
             by_axis = dict(zip(rest, index))
             if stage:
-                mine = source(i, stage)[
+                mine = partial[i][stage - 1][
                     tuple(place[axis] if a == axis else by_axis[a] for a in axes)
                 ]
             else:
@@ -286,7 +321,7 @@
 
     own = [
         pltpu.make_async_copy(
-            pick(terms[i], range(4), orders[i][0], place[orders[i][0]]),
+            pick(i, 0, range(4), orders[i][0], place[orders[i][0]]),
             partial[i][0],
             local_sem.at[i],
         )
@@ -310,12 +345,14 @@
                 flying[i].append(start(i, stage + 1))
 
 
-def scatter_sum(sizes, orders, terms):
-    count = len(terms)
+def scatter_sum(sizes, terms):
+    pieces = cut_pieces([t.shape[4] for t in terms], SCATTER_ORDERS)
+    arrays, count = len(terms), len(pieces)
     slots = sum(size - 1 for size in sizes)
     buffers = []
-    for order, term in zip(orders, terms):
-        tile = term.shape[4:]
+    for array, _, height, order in pieces:
+        term = terms[array]
+        tile = (height, term.shape[5])
         partial, landing = [], []
         for stage, axis in enumerate(order):
             rest = tuple(sizes[a] for a in range(4) if a not in order[: stage + 1])
@@ -324,10 +361,10 @@
             landing.append(pltpu.VMEM((max(sizes[axis] - 1, 1),) + rest + tile, term.dtype))
         buffers.extend(partial + landing)
     return pl.pallas_call(
-        functools.partial(scatter_kernel, sizes, orders),
+        functools.partial(scatter_kernel, sizes, pieces, arrays),
         out_shape=[jax.ShapeDtypeStruct(t.shape[4:], jnp.float32) for t in terms],
-        in_specs=[pl.BlockSpec(memory_space=pl.ANY)] * count,
-        out_specs=[pl.BlockSpec(memory_space=pltpu.VMEM)] * count,
+        in_specs=[pl.BlockSpec(memory_space=pl.ANY)] * arrays,
+        out_specs=[pl.BlockSpec(memory_space=pltpu.VMEM)] * arrays,
         scratch_shapes=buffers
         + [
             pltpu.SemaphoreType.DMA((count,)),
@@ -364,10 +401,8 @@
     width_ffn = gate_weight.shape[0]
     gain_share = norm_gains.shape[0]
     gain_tile = jnp.pad(norm_gains[None], ((0, 15), (0, -gain_share % 128)))
-    first, second = GATHER_ORDERS
     all_gains, w_query, w_kv, w_out, w_upper, w_gate, w_down = gather_all(
         sizes,
-        (second, first, second, first, second, first, second),
         (
             gain_tile,
             q_weight,
@@ -480,7 +515,7 @@
     unused, pull = jax.vjp(rms_scale, seq_inputs, gain_in)
     d_in_norm, grad_in = pull(d_normed_in)
     input_grad = d_middle + d_in_norm
-    gains_grad = jnp.concatenate([grad_in, grad_attn, grad_pre, grad_post, grad_query, grad_key])
+    gains_grad = lay_end_to_end([grad_in, grad_attn, grad_pre, grad_post, grad_query, grad_key])
 
     def grad_term(left, right):
         return outer_sum(left, right).astype(jnp.bfloat16)
@@ -498,10 +533,8 @@
     gain_term = jnp.pad(
         gains_grad.reshape(devices, 1, gain_share), ((0, 0), (0, 7), (0, -gain_share % 128))
     )
-    first, second = SCATTER_ORDERS
     gains_sum, down_sum, gate_sum, up_sum, o_sum, q_sum, kv_sum = scatter_sum(
         sizes,
-        (second, first, second, first, second, first, second),
         (
             gain_term.reshape(sizes + gain_term.shape[1:]),
             by_owner(grad_term(hidden, d_ffn)),

time: 238 us -> 223 us (0.937)
  local copies, waits for them, and re-layouts: 27.2 us -> 19.9 us
  Pallas kernels: 146 us -> 139 us
  waiting for transfers between devices: 3.93 us -> 0.01 us
    pallas_call x2, Pallas kernels: 146 us -> 139 us  [the longest x1 69.7 us: gather_all(): pl.pallas_call(functools.partial(gather_kernel, sizes, pieces, arrays), o...]
    unnamed x128 -> x113, local copies, waits for them, and re-layouts: 16.2 us -> 9.71 us
    ppermute x4, waiting for transfers between devices: 3.93 us -> 0.01 us  [shifted(): return lax.ppermute(block, axis, route)]
  transfers between devices with their start and end apart: 4 -> 4, of which waited for: 2 -> 0; matrix products, arithmetic and copies ran while one was open for 3% -> 10% of each run, Pallas kernels for 0% -> 0%
where the time goes in v2:
time: 223 us; the launch traced here: 222 us
  Pallas kernels  139 us (62%)
  matrix products  35.1 us (16%)
  local copies, waits for them, and re-layouts  19.9 us (9%)
  other arithmetic  17.5 us (8%)
  starting transfers between devices  8.68 us (4%)
    pallas_call x1, Pallas kernels, gather_all(): pl.pallas_call(functools.partial(gather_kernel, sizes, pieces, arrays), o...  69.7 us
    pallas_call x1, Pallas kernels, scatter_sum(): pl.pallas_call(functools.partial(scatter_kernel, sizes, pieces, arrays),...  69.7 us
    dot_general x9, matrix products, outer_sum(): lax.dot_general(left, right, (((0,), (0,)), ((), ())), preferred_element_...  12.7 us
    dot_general x9, matrix products, times_plain(): return jnp.dot(left, weight, preferred_element_type=jnp.float32)  12.3 us
    dot_general x9, matrix products, times_rows(): lax.dot_general(left, weight, (((1,), (1,)), ((), ())), preferred_element...  10.1 us
    unnamed x113, local copies, waits for them, and re-layouts  9.71 us
    ppermute x4, starting transfers between devices, shifted(): return lax.ppermute(block, axis, route)  8.68 us
    reduce_sum x4, other arithmetic, rms_scale(): return values * inverse * scales  4.57 us
  transfers between devices with their start and end apart: 4, of which 0 were waited for; matrix products, arithmetic and copies ran while one was open for 10% of the time, Pallas kernels for 0%

profile of v2, /device:TPU:0, one launch (start us, length us, event | category | flops | bytes accessed | tf_op | source)
XLA Modules:
  0.0 222.2 jit_solution(15818901890517142008)
XLA Ops:
  0.7 1.1 fusion.21
  1.8 1.3 pad.44.refs_0_
  3.0 1.3 pad_maximum_fusion.8.refs_2_
  4.4 69.7 %gather_all.1 = (bf16[4,2,2,2,16,128]{5,4,3,2,1,0:T(8,128)(2,1)}, bf16[4,2,2,2,32,640]{5,4,3,2,1,0:T(8,128)(2,1)}, bf16[4,2,2,2,16,640]{5,4,3,2,1,0:T(8,128)(2,1...) custom-call(bf16[16,128]{1,0:T(8,128)(2,1)} %pad.44.refs_0_, ...), custom_call_target="tpu_custom_call" | custom-call | tf_op jit(solution)/shard_map/gather_all/pallas_call | solution.py:229
  74.1 1.0 fusion.49
  75.2 0.6 fusion.67
  75.8 1.1 multiply_convert_fusion.4
  76.8 1.9 convolution_convert_fusion.9
  78.8 4.0 %collective-permute-start.1 = (bf16[128,256]{1,0:T(8,128)(2,1)}, bf16[128,256]{1,0:T(8,128)(2,1)}, u32[]{:S(2)}, u32[]{:S(2)}) collective-permute-start(bf16[128,256]{1,0:T(8,128)(2,1)} %convolution_convert_fusion.9), channel_id=1, source_target_pairs={{0,1},{2,3},{4,5},{6,7},{8,9},{10,11},{12,13},{14,15},{16,17},{18,... | collective-permute-start | bytes 196616 | tf_op jit(solution)/shard_map/ppermute | solution.py:22
  82.8 1.3 multiply_reduce_fusion.13
  84.9 1.9 collective-permute-start
  86.8 0.6 multiply_reduce_fusion.3
  88.3 1.2 fusion.69
  89.6 0.6 copy-done.6
  90.3 2.1 convolution_convert_fusion.8
  92.3 1.8 copy.25
  94.1 1.9 multiply_reduce_fusion.12
  96.4 1.0 fusion.70
  97.8 1.0 multiply_convert_fusion.1
  98.8 0.7 copy-done.17
  99.5 0.7 multiply_reduce_fusion.10
  100.2 0.7 fusion.20
  100.9 0.9 fusion.15
  101.8 1.4 multiply_convert_fusion
  103.2 0.6 fusion.71
  103.8 1.2 multiply_reduce_fusion.4
  105.1 0.8 multiply_reduce_fusion.5
  105.9 0.7 copy-done.15
  106.7 0.5 convolution_convert_fusion.7
  107.3 1.6 convolution_convert_fusion.4
  108.9 2.4 %convolution_convert_fusion = bf16[2048,640]{1,0:T(8,128)(2,1)} fusion(bf16[128,2048]{1,0:T(8,128)(2,1)S(1)} %get-tuple-element.57, bf16[128,640]{1,0:T(8,128)(2,1)S(1)} %multiply_convert_fusion.3), kind=kOutput, calls=%fused_computation | convolution fusion | flops 336855040 | bytes 3309568 | tf_op jit(solution)/shard_map/dot_general | solution.py:86
  111.3 0.9 convolution_convert_fusion.1
  112.2 2.4 %convolution_convert_fusion.2 = bf16[2048,640]{1,0:T(8,128)(2,1)} fusion(bf16[128,2048]{1,0:T(8,128)(2,1)S(1)} %get-tuple-element.89, bf16[128,640]{1,0:T(8,128)(2,1)S(1)} %get-tuple-element.63), kind=kOutput, calls=%fused_computation.2 | convolution fusion | flops 336855040 | bytes 3309568 | tf_op jit(solution)/shard_map/dot_general | solution.py:86
  115.1 1.2 fusion.2
  116.6 0.7 copy-done.21
  117.2 0.6 slice.127
  117.9 0.6 slice.126
  118.5 1.3 collective-permute-start.3
  119.8 1.5 collective-permute-start.2
  121.3 1.9 convolution_multiply_fusion
  123.3 2.0 copy.29
  125.3 1.2 multiply_bitcast_fusion
  126.5 1.9 multiply_reduce_fusion
  128.4 0.9 fusion.10
  129.3 1.8 copy.30
  131.2 2.6 %convolution_convert_fusion.3 = bf16[1024,640]{1,0:T(8,128)(2,1)} fusion(bf16[128,1024]{0,1:T(8,128)(2,1)} %bitcast.201, bf16[1,128,640]{2,1,0:T(8,128)(2,1)} %copy-done.10), kind=kOutput, calls=%fused_computation.3 | convolution fusion | flops 168427520 | bytes 1736704 | tf_op jit(solution)/shard_map/dot_general | solution.py:86
  133.8 1.8 fusion.72
  135.7 1.4 multiply_bitcast_fusion.1
  137.2 1.2 fusion.38
  138.7 1.0 convolution_convert_fusion.6
  139.8 1.8 multiply_reduce_fusion.6
  141.8 1.3 convolution_convert_fusion.5
  143.1 1.0 pad_maximum_fusion.refs_6_
  144.2 1.7 copy-done
  145.9 1.3 copy-done.2
  147.3 69.7 %scatter_sum.1 = (f32[8,128]{1,0:T(8,128)S(1)}, f32[64,640]{1,0:T(8,128)S(1)}, f32[64,640]{1,0:T(8,128)S(1)}, f32[64,640]{1,0:T(8,128)S(1)}, f32[32,640]{1,0:T(8...) custom-call(f32[4,2,2,2,8,128]{5,4,3,2,1,0:T(8,128)S(1)} %bitcast.182, ...), custom_call_target="tpu_custom_call" | custom-call | tf_op jit(solution)/shard_map/scatter_sum/pallas_call | solution.py:363
  217.0 0.5 slice_bitcast_fusion.7
  217.5 0.6 fusion.66
  218.1 0.9 fusion.19
  219.0 0.6 copy.43
  219.6 0.6 copy.44
  220.2 0.7 copy.45
  220.9 0.7 copy.46
  221.6 0.7 copy.47
  (150 shorter events, 3.9 us)
Async XLA Ops:
  0.6 83.6 %copy-start.49 = (s32[1,256]{1,0:T(1,128)S(1)}, s32[1,256]{1,0:T(1,128)}, u32[]{:S(2)}) copy-start(s32[1,256]{1,0:T(1,128)} %param.12) | copy-start | bytes 3076
  1.7 81.0 %copy-start.50 = (f32[128]{0:T(128)}, f32[128]{0:T(128)S(1)}, u32[]{:S(2)}) copy-start(f32[128]{0:T(128)S(1)} %fusion.21) | copy-start | bytes 1540
  1.8 81.0 %copy-start.44 = (f32[128]{0:T(128)}, f32[128]{0:T(128)S(1)}, u32[]{:S(2)}) copy-start(f32[128]{0:T(128)S(1)} %fusion.51) | copy-start | bytes 1540
  74.1 12.8 %copy-start.8 = (bf16[4,2,2,2,32,640]{5,4,3,2,1,0:T(8,128)(2,1)S(1)}, bf16[4,2,2,2,32,640]{5,4,3,2,1,0:T(8,128)(2,1)}, u32[]{:S(2)}) copy-start(bf16[4,2,2,2,32,640]{5,4,3,2,1,0:T(8,128)(2,1)} %get-tuple-element.25) | copy-start | bytes 3932164
  76.8 10.8 %copy-start.10 = (bf16[1,128,640]{2,1,0:T(8,128)(2,1)}, bf16[1,128,640]{2,1,0:T(8,128)(2,1)S(1)}, u32[]{:S(2)}) copy-start(bf16[1,128,640]{2,1,0:T(8,128)(2,1)S(1)} %multiply_convert_fusion.4) | copy-start | bytes 491524
  78.8 10.9 %collective-permute-start.1 = (bf16[128,256]{1,0:T(8,128)(2,1)}, bf16[128,256]{1,0:T(8,128)(2,1)}, u32[]{:S(2)}, u32[]{:S(2)}) collective-permute-start(bf16[128,256]{1,0:T(8,128)(2,1)} %convolution_convert_fusion.9), channel_id=1, source_target_pairs={{0,1},{2,3},{4,5},{6,7},{8,9},{10,11},{12,13},{14,15},{16,17},{18,... | collective-permute-start | bytes 196616 | tf_op jit(solution)/shard_map/ppermute | solution.py:22
  82.8 4.9 %copy-start.35 = (f32[256]{0:T(256)}, f32[256]{0:T(256)S(1)}, u32[]{:S(2)}) copy-start(f32[256]{0:T(256)S(1)} %get-tuple-element.78) | copy-start | bytes 3076
  82.8 5.0 %copy-start.37 = (f32[256]{0:T(256)}, f32[256]{0:T(256)S(1)}, u32[]{:S(2)}) copy-start(f32[256]{0:T(256)S(1)} %get-tuple-element.79) | copy-start | bytes 3076
  84.1 3.6 %copy-start.12 = (f32[128,256]{1,0:T(8,128)}, f32[128,256]{1,0:T(8,128)S(1)}, u32[]{:S(2)}) copy-start(f32[128,256]{1,0:T(8,128)S(1)} %get-tuple-element.84) | copy-start | bytes 393220
  84.1 3.6 %copy-start.52 = (f32[128]{0:T(128)}, f32[128]{0:T(128)S(1)}, u32[]{:S(2)}) copy-start(f32[128]{0:T(128)S(1)} %get-tuple-element.83) | copy-start | bytes 1540
  84.1 3.6 %copy-start.46 = (f32[128]{0:T(128)}, f32[128]{0:T(128)S(1)}, u32[]{:S(2)}) copy-start(f32[128]{0:T(128)S(1)} %fusion.52) | copy-start | bytes 1540
  84.9 3.1 %copy-start.26 = (f32[128,256]{1,0:T(8,128)}, f32[128,256]{1,0:T(8,128)S(1)}, u32[]{:S(2)}) copy-start(f32[128,256]{1,0:T(8,128)S(1)} %get-tuple-element.71) | copy-start | bytes 393220
  84.9 3.0 %copy-start.27 = (f32[128,256]{1,0:T(8,128)}, f32[128,256]{1,0:T(8,128)S(1)}, u32[]{:S(2)}) copy-start(f32[128,256]{1,0:T(8,128)S(1)} %get-tuple-element.70) | copy-start | bytes 393220
  84.9 3.4 %copy-start.30 = (bf16[128,256]{1,0:T(8,128)(2,1)}, bf16[128,256]{1,0:T(8,128)(2,1)S(1)}, u32[]{:S(2)}) copy-start(bf16[128,256]{1,0:T(8,128)(2,1)S(1)} %get-tuple-element.69) | copy-start | bytes 196612
  84.9 3.2 %collective-permute-start = (bf16[128,256]{1,0:T(8,128)(2,1)S(1)}, bf16[128,256]{1,0:T(8,128)(2,1)}, u32[]{:S(2)}, u32[]{:S(2)}) collective-permute-start(bf16[128,256]{1,0:T(8,128)(2,1)S(1)} %get-tuple-element.69), channel_id=1, source_target_pairs={{0,1},{2,3},{4,5},{6,7},{8,9},{10,11},{12,13},{14,15},{16,17},{18,... | collective-permute-start | bytes 196616 | tf_op jit(solution)/shard_map/ppermute | solution.py:22
  87.5 0.8 copy-start.39
  87.9 1.5 copy-start.28
  88.3 7.7 %copy-start.3 = (f32[1,128,640]{2,1,0:T(8,128)S(1)}, f32[1,128,640]{2,1,0:T(8,128)}, u32[]{:S(2)}) copy-start(f32[1,128,640]{2,1,0:T(8,128)} %param.11) | copy-start | bytes 983044
  89.5 0.8 copy-start.6
  89.5 6.9 %copy-start.5 = (bf16[4,2,2,2,64,640]{5,4,3,2,1,0:T(8,128)(2,1)S(1)}, bf16[4,2,2,2,64,640]{5,4,3,2,1,0:T(8,128)(2,1)}, u32[]{:S(2)}) copy-start(bf16[4,2,2,2,64,640]{5,4,3,2,1,0:T(8,128)(2,1)} %get-tuple-element.28) | copy-start | bytes 7864324
  89.6 2.7 %copy-start.33 = (f32[512]{0:T(512)}, f32[512]{0:T(512)S(1)}, u32[]{:S(2)}) copy-start(f32[512]{0:T(512)S(1)} %log_add_fusion) | copy-start | bytes 6148
  96.0 1.7 copy-start.4
  97.8 1.7 copy-start.17
  98.8 1.4 copy-start.14
  98.8 1.4 copy-start.32
  103.8 2.9 %copy-start.9 = (bf16[4,2,2,2,32,640]{5,4,3,2,1,0:T(8,128)(2,1)S(1)}, bf16[4,2,2,2,32,640]{5,4,3,2,1,0:T(8,128)(2,1)}, u32[]{:S(2)}) copy-start(bf16[4,2,2,2,32,640]{5,4,3,2,1,0:T(8,128)(2,1)} %get-tuple-element.27) | copy-start | bytes 3932164
  105.0 2.2 %copy-start.19 = (bf16[4,128,256]{1,2,0:T(8,128)(2,1)S(1)}, bf16[4,128,256]{1,2,0:T(8,128)(2,1)}, u32[]{:S(2)}) copy-start(bf16[4,128,256]{1,2,0:T(8,128)(2,1)} %copy.25) | copy-start | bytes 786436
  105.9 0.7 copy-start.15
  112.1 2.5 %copy-start.18 = (bf16[512,256]{1,0:T(8,128)(2,1)S(1)}, bf16[512,256]{1,0:T(8,128)(2,1)}, u32[]{:S(2)}) copy-start(bf16[512,256]{1,0:T(8,128)(2,1)} %convolution_convert_fusion.8) | copy-start | bytes 786436
  112.1 2.6 %copy-start.7 = (f32[512,256]{0,1:T(8,128)S(1)}, f32[512,256]{0,1:T(8,128)}, u32[]{:S(2)}) copy-start(f32[512,256]{0,1:T(8,128)} %copy-done.6) | copy-start | bytes 1572868
  112.2 2.6 %copy-start.34 = (f32[512]{0:T(512)S(1)}, f32[512]{0:T(512)}, u32[]{:S(2)}) copy-start(f32[512]{0:T(512)} %copy-done.33) | copy-start | bytes 6148
  112.2 4.1 %copy-start.29 = (bf16[128,4,256]{2,0,1:T(8,128)(2,1)S(1)}, bf16[128,4,256]{2,0,1:T(8,128)(2,1)}, u32[]{:S(2)}) copy-start(bf16[128,4,256]{2,0,1:T(8,128)(2,1)} %copy-done.28) | copy-start | bytes 786436
  114.6 6.8 %copy-start.31 = (bf16[128,256]{1,0:T(8,128)(2,1)S(1)}, bf16[128,256]{1,0:T(8,128)(2,1)}, u32[]{:S(2)}) copy-start(bf16[128,256]{1,0:T(8,128)(2,1)} %copy-done.30) | copy-start | bytes 196612
  115.0 2.8 %copy-start.23 = (f32[256,256]{1,0:T(8,128)}, f32[256,256]{1,0:T(8,128)S(1)}, u32[]{:S(2)}) copy-start(f32[256,256]{1,0:T(8,128)S(1)} %fusion.44) | copy-start | bytes 786436
  116.3 10.2 %copy-start.38 = (f32[256]{0:T(256)S(1)}, f32[256]{0:T(256)}, u32[]{:S(2)}) copy-start(f32[256]{0:T(256)} %copy-done.37) | copy-start | bytes 3076
  116.6 0.7 copy-start.21
  118.5 21.3 %collective-permute-start.3 = (bf16[128,256]{1,0:T(8,128)(2,1)}, bf16[128,256]{1,0:T(8,128)(2,1)}, u32[]{:S(2)}, u32[]{:S(2)}) collective-permute-start(bf16[128,256]{1,0:T(8,128)(2,1)} %slice.126), channel_id=1, source_target_pairs={{1,0},{3,2},{5,4},{7,6},{9,8},{11,10},{13,12},{15,14},{17,16},{19,... | collective-permute-start | bytes 196616 | tf_op jit(solution)/shard_map/ppermute | solution.py:22
  119.8 15.9 %collective-permute-start.2 = (bf16[128,256]{1,0:T(8,128)(2,1)}, bf16[128,256]{1,0:T(8,128)(2,1)}, u32[]{:S(2)}, u32[]{:S(2)}) collective-permute-start(bf16[128,256]{1,0:T(8,128)(2,1)} %slice.127), channel_id=1, source_target_pairs={{1,0},{3,2},{5,4},{7,6},{9,8},{11,10},{13,12},{15,14},{17,16},{19,... | collective-permute-start | bytes 196616 | tf_op jit(solution)/shard_map/ppermute | solution.py:22
  123.3 5.1 %copy-start.40 = (f32[128,4]{0,1:T(4,128)S(1)}, f32[128,4]{0,1:T(4,128)}, u32[]{:S(2)}) copy-start(f32[128,4]{0,1:T(4,128)} %copy-done.39) | copy-start | bytes 6148
  129.3 7.8 %copy-start.13 = (f32[128,256]{1,0:T(8,128)S(1)}, f32[128,256]{1,0:T(8,128)}, u32[]{:S(2)}) copy-start(f32[128,256]{1,0:T(8,128)} %copy-done.12) | copy-start | bytes 393220
  129.3 7.8 %copy-start.36 = (f32[256]{0:T(256)S(1)}, f32[256]{0:T(256)}, u32[]{:S(2)}) copy-start(f32[256]{0:T(256)} %copy-done.35) | copy-start | bytes 3076
  129.3 7.8 %copy-start.47 = (f32[128]{0:T(128)S(1)}, f32[128]{0:T(128)}, u32[]{:S(2)}) copy-start(f32[128]{0:T(128)} %copy-done.46) | copy-start | bytes 1540
  129.3 9.0 %copy-start.53 = (f32[128]{0:T(128)S(1)}, f32[128]{0:T(128)}, u32[]{:S(2)}) copy-start(f32[128]{0:T(128)} %copy-done.52) | copy-start | bytes 1540
  131.1 6.0 %copy-start.22 = (f32[256,256]{1,0:T(8,128)S(1)}, f32[256,256]{1,0:T(8,128)}, u32[]{:S(2)}) copy-start(f32[256,256]{1,0:T(8,128)} %copy-done.21) | copy-start | bytes 786436
  131.2 7.3 %copy-start.20 = (bf16[4,2,2,2,16,640]{5,4,3,2,1,0:T(8,128)(2,1)S(1)}, bf16[4,2,2,2,16,640]{5,4,3,2,1,0:T(8,128)(2,1)}, u32[]{:S(2)}) copy-start(bf16[4,2,2,2,16,640]{5,4,3,2,1,0:T(8,128)(2,1)} %get-tuple-element.26) | copy-start | bytes 1966084
  133.8 4.9 %copy-start.11 = (bf16[1,128,640]{2,1,0:T(8,128)(2,1)S(1)}, bf16[1,128,640]{2,1,0:T(8,128)(2,1)}, u32[]{:S(2)}) copy-start(bf16[1,128,640]{2,1,0:T(8,128)(2,1)} %copy-done.10) | copy-start | bytes 491524
  133.8 6.0 %copy-start.24 = (f32[256,256]{1,0:T(8,128)S(1)}, f32[256,256]{1,0:T(8,128)}, u32[]{:S(2)}) copy-start(f32[256,256]{1,0:T(8,128)} %copy-done.23) | copy-start | bytes 786436
  133.8 6.0 %copy-start.45 = (f32[128]{0:T(128)S(1)}, f32[128]{0:T(128)}, u32[]{:S(2)}) copy-start(f32[128]{0:T(128)} %copy-done.44) | copy-start | bytes 1540
  135.6 6.0 %copy-start.51 = (f32[128]{0:T(128)S(1)}, f32[128]{0:T(128)}, u32[]{:S(2)}) copy-start(f32[128]{0:T(128)} %copy-done.50) | copy-start | bytes 1540
  135.7 6.0 %copy-start.41 = (f32[640]{0:T(1024)S(1)}, f32[640]{0:T(1024)}, u32[]{:S(2)}) copy-start(f32[640]{0:T(1024)} %get-tuple-element.44) | copy-start | bytes 7684
  135.7 6.0 %copy-start.42 = (f32[640]{0:T(1024)S(1)}, f32[640]{0:T(1024)}, u32[]{:S(2)}) copy-start(f32[640]{0:T(1024)} %get-tuple-element.42) | copy-start | bytes 7684
  135.7 6.0 %copy-start.43 = (f32[640]{0:T(1024)S(1)}, f32[640]{0:T(1024)}, u32[]{:S(2)}) copy-start(f32[640]{0:T(1024)} %get-tuple-element.46) | copy-start | bytes 7684
  135.7 6.0 %copy-start.48 = (f32[256]{0:T(256)S(1)}, f32[256]{0:T(256)}, u32[]{:S(2)}) copy-start(f32[256]{0:T(256)} %get-tuple-element.38) | copy-start | bytes 3076
  141.8 2.4 %copy-start.1 = (bf16[1024,640]{1,0:T(8,128)(2,1)S(1)}, bf16[1024,640]{1,0:T(8,128)(2,1)}, u32[]{:S(2)}) copy-start(bf16[1024,640]{1,0:T(8,128)(2,1)} %convolution_convert_fusion.4) | copy-start | bytes 3932164
  144.2 1.7 copy-start
  145.9 1.3 copy-start.2
  147.2 70.8 %copy-start.16 = (f32[128,640]{1,0:T(8,128)S(1)}, f32[128,640]{1,0:T(8,128)}, u32[]{:S(2)}) copy-start(f32[128,640]{1,0:T(8,128)} %copy-done.15) | copy-start | bytes 983044
  147.3 70.8 %copy-start.25 = (f32[128,640]{1,0:T(8,128)S(1)}, f32[128,640]{1,0:T(8,128)}, u32[]{:S(2)}) copy-start(f32[128,640]{1,0:T(8,128)} %get-tuple-element.94) | copy-start | bytes 983044
